TPU v7x, 512 devices: a whole 4x4x16 slice. The times are simulated.
512 devices in a mesh: row: 16 (over x_hi, y, core), col: 32 (over z, x_lo).
Axes of the slice: x: 4 (x_hi: 2, x_lo: 2; x = x_hi * 2 + x_lo), y: 4, z: 16, core: 2. Of those that a mesh axis runs over, the one named last changes fastest.
Arguments:
- volume: float32 [8, 4096, 4096], P(None, 'row', 'col'), may hold values from -6 to 6
- ray_weights: float32 [64, 4096], P(None, 'row'), may hold values from 0.5 to 2
- shear_weights: bfloat16 [64, 128, 128], replicated, may hold values from -0.5 to 0.5
- shear_offsets: int32 [64], replicated, may hold values from 0 to 31
- measured: float32 [64, 8, 4096], P('row', None, 'col'), may hold values from -6 to 6
Outputs:
- residual: float32 [64, 8, 4096], P('row', None, 'col')
- gradient: float32 [8, 4096, 4096], P(None, 'row', 'col')
All inputs are finite; a program needn't handle non-finite values.
Results may differ from a plain program's by a relative error of at most 0.0003.
Values sent between devices are 32-bit elements; how exact they have to be, the bound alone decides.
No kernel may reach another device: no remote copies, remote signals or barrier semaphores. Data moves between devices by JAX's collectives and lax.ppermute only.
A program may use at most 64 MiB of HBM per device.

v0:
```python
import math

import jax
import jax.numpy as jnp
from jax import lax
from jax.sharding import PartitionSpec as P


def rotate_cols(values, amounts, sign):
    col_count = lax.axis_size("col")
    shape = values.shape
    pieces = values.reshape(shape[0], col_count, -1)
    spread_out = lax.all_to_all(pieces, "col", split_axis=1, concat_axis=1, tiled=True)
    slots = jnp.arange(col_count, dtype=jnp.int32)
    source = (slots[None, :] - sign * amounts[:, None]) % col_count
    reordered = jnp.take_along_axis(spread_out, source[:, :, None], axis=1)
    settled = lax.all_to_all(reordered, "col", split_axis=1, concat_axis=1, tiled=True)
    return settled.reshape(shape)


def push_cols(values, amounts):
    return rotate_cols(values, amounts, 1)


def pull_cols(values, amounts):
    return rotate_cols(values, amounts, -1)


def on_device(volume, ray_weights, shear_weights, shear_offsets, measured):
    highest = lax.Precision.HIGHEST
    row_count = lax.axis_size("row")
    col_count = lax.axis_size("col")
    row_index = lax.axis_index("row")
    slab_rows = volume.shape[1]
    per_owner = measured.shape[0]
    factor = 1.0 / math.sqrt(slab_rows * row_count)
    shear = shear_weights.astype(jnp.float32)
    owned = lax.dynamic_slice_in_dim(shear, row_index * per_owner, per_owner, 0)
    offsets_owned = lax.dynamic_slice_in_dim(shear_offsets, row_index * per_owner, per_owner, 0)
    tilesum = jnp.einsum("ax,sxy->asy", ray_weights, volume, precision=highest) * factor
    received = lax.all_to_all(tilesum, "row", split_axis=0, concat_axis=0, tiled=True)
    sources = jnp.arange(received.shape[0], dtype=jnp.int32) // per_owner
    amounts = jnp.tile(offsets_owned, row_count) * sources % col_count
    landed = push_cols(received, amounts)
    projection = jnp.sum(landed.reshape((row_count, per_owner) + landed.shape[1:]), axis=0)
    projection = jnp.einsum("asy,ayz->asz", projection, owned, precision=highest)
    residual = projection - measured
    returning = jnp.einsum("asz,ayz->asy", residual, owned, precision=highest)
    copies = jnp.tile(returning, (row_count, 1, 1))
    shifted = pull_cols(copies, amounts)
    arrived = lax.all_to_all(shifted, "row", split_axis=0, concat_axis=0, tiled=True)
    gradient = jnp.einsum("ax,asy->sxy", ray_weights, arrived, precision=highest) * factor
    return (residual, gradient)


def solution(mesh):
    placed = (P(None, "row", "col"), P(None, "row"), P(), P(), P("row", None, "col"))
    return jax.shard_map(
        on_device,
        mesh=mesh,
        in_specs=placed,
        out_specs=(P("row", None, "col"), P(None, "row", "col")),
        check_vma=False,
    )
```

profile of v0, /device:TPU:1, one launch (start us, length us, event | category | flops | bytes accessed | tf_op | source)
XLA Modules:
  0.0 216.0 jit_solution(18437675435340744423)
XLA Ops:
  0.7 2.2 convolution_multiply_fusion.1
  3.0 18.0 %all_to_all.30 = f32[64,8,128]{2,1,0:T(8,128)S(1)} all-to-all(f32[64,8,128]{2,1,0:T(8,128)S(1)} %copy.15), channel_id=1, replica_groups=mesh['row'=16,'col'=32] {'row'}, dimensions={0} | all-to-all | bytes 524288 | tf_op jit(solution)/shard_map/all_to_all | solution.py:41
  21.2 1.0 reshape.201
  22.3 14.1 %all-to-all-start.1 = ((f32[32,1,2048]{2,1,0:T(1,128)}), f32[32,1,2048]{2,1,0:T(1,128)S(1)}, u32[]{:S(2)}, u32[]{:S(2)}) async-start(f32[32,1,2048]{2,1,0:T(1,128)} %reshape.201), calls=%async_computation.1 | async-start | bytes 524288 | tf_op jit(solution)/shard_map/all_to_all | solution.py:13
  37.0 18.9 %all-to-all-done.1 = f32[32,1,2048]{2,1,0:T(1,128)S(1)} async-done(((f32[32,1,2048]{2,1,0:T(1,128)}), f32[32,1,2048]{2,1,0:T(1,128)S(1)}, u32[]{:S(2)}, u32[]{:S(2)}) %all-to-all-start.1) | async-done | bytes 262176 | tf_op jit(solution)/shard_map/all_to_all | solution.py:13
  55.9 0.6 broadcast.284
  56.5 1.2 reduce
  57.7 1.0 reshape.202
  58.7 1.9 copy.17
  60.6 22.7 %gather_fusion = f32[2048,32]{1,0:T(8,128)} fusion(f32[64,32,32]{2,1,0:T(8,128)S(1)} %copy.17, s32[2048]{0:T(1024)S(1)} %reshape.192), kind=kCustom, calls=%fused_computation.clone | custom fusion | bytes 540672 | tf_op jit(solution)/shard_map/jit(take_along_axis)/gather | solution.py:16
  83.3 1.8 copy.18
  85.1 0.3 reshape.203
  85.5 23.9 %all_to_all.31 = f32[32,1,2048]{2,1,0:T(1,128)S(1)} all-to-all(f32[32,1,2048]{2,1,0:T(1,128)S(1)} %reshape.203), channel_id=1, replica_groups=mesh['row'=16,'col'=32] {'col'}, dimensions={0} | all-to-all | bytes 524288 | tf_op jit(solution)/shard_map/all_to_all | solution.py:17
  109.3 1.2 reduce.1
  110.6 1.0 reshape.204
  111.6 2.0 copy.19
  114.1 0.3 fusion.2
  114.7 1.4 copy.21
  116.1 2.1 reshape.205
  118.2 5.3 %all-to-all-start.3 = ((f32[32,1,2048]{2,1,0:T(1,128)}), f32[32,1,2048]{2,1,0:T(1,128)S(1)}, u32[]{:S(2)}, u32[]{:S(2)}) async-start(f32[32,1,2048]{2,1,0:T(1,128)} %reshape.205), calls=%async_computation.3 | async-start | bytes 524288 | tf_op jit(solution)/shard_map/all_to_all | solution.py:13
  123.8 18.3 %all-to-all-done.3 = f32[32,1,2048]{2,1,0:T(1,128)S(1)} async-done(((f32[32,1,2048]{2,1,0:T(1,128)}), f32[32,1,2048]{2,1,0:T(1,128)S(1)}, u32[]{:S(2)}, u32[]{:S(2)}) %all-to-all-start.3) | async-done | bytes 262176 | tf_op jit(solution)/shard_map/all_to_all | solution.py:13
  142.1 1.2 reduce.2
  143.3 1.0 reshape.206
  144.4 1.9 copy.22
  146.2 22.7 %gather_fusion.1 = f32[2048,32]{1,0:T(8,128)} fusion(f32[64,32,32]{2,1,0:T(8,128)S(1)} %copy.22, s32[2048]{0:T(1024)S(1)} %reshape.196), kind=kCustom, calls=%fused_computation.1.clone | custom fusion | bytes 540672 | tf_op jit(solution)/shard_map/jit(take_along_axis)/gather | solution.py:16
  168.9 1.8 copy.23
  170.8 0.3 reshape.207
  171.1 24.2 %all_to_all.32 = f32[32,1,2048]{2,1,0:T(1,128)S(1)} all-to-all(f32[32,1,2048]{2,1,0:T(1,128)S(1)} %reshape.207), channel_id=1, replica_groups=mesh['row'=16,'col'=32] {'col'}, dimensions={0} | all-to-all | bytes 524288 | tf_op jit(solution)/shard_map/all_to_all | solution.py:17
  195.2 1.2 reduce.3
  196.9 16.7 %all_to_all.33 = f32[64,8,128]{2,1,0:T(8,128)S(1)} all-to-all(f32[64,8,128]{2,1,0:T(8,128)S(1)} %copy.24), channel_id=1, replica_groups=mesh['row'=16,'col'=32] {'row'}, dimensions={0} | all-to-all | bytes 524288 | tf_op jit(solution)/shard_map/all_to_all | solution.py:51
  213.7 1.0 fusion
  214.7 1.3 copy.26
  (32 shorter events, 2.6 us)
Async XLA Ops:
  0.6 113.2 %copy-start = (bf16[64,128,128]{2,1,0:T(8,128)(2,1)S(1)}, bf16[64,128,128]{2,1,0:T(8,128)(2,1)}, u32[]{:S(2)}) copy-start(bf16[64,128,128]{2,1,0:T(8,128)(2,1)} %param.9) | copy-start | bytes 6291460
  0.6 35.7 %copy-start.4 = (s32[64]{0:T(128)S(1)}, s32[64]{0:T(128)}, u32[]{:S(2)}) copy-start(s32[64]{0:T(128)} %param.10) | copy-start | bytes 772
  22.3 33.6 %all-to-all-start.1 = ((f32[32,1,2048]{2,1,0:T(1,128)}), f32[32,1,2048]{2,1,0:T(1,128)S(1)}, u32[]{:S(2)}, u32[]{:S(2)}) async-start(f32[32,1,2048]{2,1,0:T(1,128)} %reshape.201), calls=%async_computation.1 | async-start | bytes 524288 | tf_op jit(solution)/shard_map/all_to_all | solution.py:13
  110.6 3.3 %copy-start.3 = (f32[4,8,128]{2,1,0:T(8,128)S(1)}, f32[4,8,128]{2,1,0:T(8,128)}, u32[]{:S(2)}) copy-start(f32[4,8,128]{2,1,0:T(8,128)} %param.11) | copy-start | bytes 49156
  114.1 4.1 %copy-start.2 = (f32[4,8,128]{2,1,0:T(8,128)}, f32[4,8,128]{2,1,0:T(8,128)S(1)}, u32[]{:S(2)}) copy-start(f32[4,8,128]{2,1,0:T(8,128)S(1)} %convolution_subtract_fusion) | copy-start | bytes 49156
  118.2 23.9 %all-to-all-start.3 = ((f32[32,1,2048]{2,1,0:T(1,128)}), f32[32,1,2048]{2,1,0:T(1,128)S(1)}, u32[]{:S(2)}, u32[]{:S(2)}) async-start(f32[32,1,2048]{2,1,0:T(1,128)} %reshape.205), calls=%async_computation.3 | async-start | bytes 524288 | tf_op jit(solution)/shard_map/all_to_all | solution.py:13
  170.7 42.9 %copy-start.1 = (f32[64,256]{1,0:T(8,128)S(1)}, f32[64,256]{1,0:T(8,128)}, u32[]{:S(2)}) copy-start(f32[64,256]{1,0:T(8,128)} %param.8) | copy-start | bytes 196612
where the time goes:
time: 217 us; the launch traced here: 216 us
  blocking collectives  82.8 us (38%)
  local copies, waits for them, and re-layouts  66.5 us (31%)
  waiting for transfers between devices  37.2 us (17%)
  starting transfers between devices  19.4 us (9%)
  other arithmetic  5.45 us (3%)
  matrix products  3.71 us (2%)
    gather x6, local copies, waits for them, and re-layouts, rotate_cols(): reordered = jnp.take_along_axis(spread_out, source[:, :, None], axis=1)  49 us
    all_to_all x2, blocking collectives, rotate_cols(): lax.all_to_all(reordered, 'col', split_axis=1, concat_axis=1, tiled=True)  48 us
    all_to_all x2, waiting for transfers between devices, rotate_cols(): lax.all_to_all(pieces, 'col', split_axis=1, concat_axis=1, tiled=True)  37.2 us
    all_to_all x2, starting transfers between devices, rotate_cols(): lax.all_to_all(pieces, 'col', split_axis=1, concat_axis=1, tiled=True)  19.4 us
    all_to_all x1, blocking collectives, on_device(): lax.all_to_all(tilesum, 'row', split_axis=0, concat_axis=0, tiled=True)  18 us
    all_to_all x1, blocking collectives, on_device(): lax.all_to_all(shifted, 'row', split_axis=0, concat_axis=0, tiled=True)  16.7 us
    unnamed x19, local copies, waits for them, and re-layouts  8.32 us
    all_to_all x3, local copies, waits for them, and re-layouts, rotate_cols(): lax.all_to_all(pieces, 'col', split_axis=1, concat_axis=1, tiled=True)  4.34 us
  transfers between devices with their start and end apart: 2, of which 2 were waited for; matrix products, arithmetic and copies ran while one was open for 0% of the time, Pallas kernels for 0%

commit v1 on v0

v1 whole, which is shorter than its diff:
```python
import math

import jax
import jax.numpy as jnp
from jax import lax
from jax.experimental import pallas as pl
from jax.experimental.pallas import tpu as pltpu
from jax.sharding import PartitionSpec as P

VMEM = pl.BlockSpec(memory_space=pltpu.VMEM)
SMEM = pl.BlockSpec(memory_space=pltpu.SMEM)


def to_lines(rows, lines, tiles_ref, extra_ref, out_ref):
    for r in range(rows):
        out_ref[pl.ds(r, lines, stride=rows + 1), :] = tiles_ref[r * lines : (r + 1) * lines, :]
    out_ref[pl.ds(rows, lines, stride=rows + 1), :] = extra_ref[...]


def to_tiles(rows, lines, in_ref, tiles_ref, extra_ref):
    for r in range(rows):
        tiles_ref[r * lines : (r + 1) * lines, :] = in_ref[pl.ds(r, lines, stride=rows + 1), :]
    extra_ref[...] = in_ref[pl.ds(rows, lines, stride=rows + 1), :]


def halves(values):
    high = values.astype(jnp.bfloat16)
    low = (values - high.astype(jnp.float32)).astype(jnp.bfloat16)
    return jnp.concatenate([high, low], axis=0)


def middle(rows, cols, factor, offset_ref, in_ref, shear_ref, out_ref, sum_ref, twice_ref):
    offset = offset_ref[0]
    sum_ref[...] = jnp.zeros_like(sum_ref)
    for r in range(rows):
        at = lax.rem(offset * r, cols)
        window = pl.ds(at, cols)
        sum_ref[window, :] = sum_ref[window, :] + in_ref[pl.ds(r, cols, stride=rows + 1), :]
    total = (sum_ref[:cols, :] + sum_ref[cols:, :]) * factor
    shear = shear_ref[...]
    both = lax.dot_general(halves(total), shear, (((1,), (0,)), ((), ())), preferred_element_type=jnp.float32)
    residual = both[:cols] + both[cols:] - in_ref[pl.ds(rows, cols, stride=rows + 1), :]
    both = lax.dot_general(halves(residual), shear, (((1,), (1,)), ((), ())), preferred_element_type=jnp.float32)
    returning = both[:cols] + both[cols:]
    twice_ref[:cols, :] = returning
    twice_ref[cols:, :] = returning
    for r in range(rows):
        at = lax.rem(offset * r, cols)
        out_ref[pl.ds(r, cols, stride=rows + 1), :] = twice_ref[pl.ds(at, cols), :]
    out_ref[pl.ds(rows, cols, stride=rows + 1), :] = residual


def exchange(values, axis):
    rows, lanes = values.shape
    return lax.all_to_all(values.reshape(rows, 1, lanes), axis, 0, 0, tiled=True).reshape(rows, lanes)


def on_device(volume, ray_weights, shear_weights, shear_offsets, measured):
    highest = lax.Precision.HIGHEST
    rows = lax.axis_size("row")
    cols = lax.axis_size("col")
    slices, slab_rows, lanes = volume.shape
    angles = ray_weights.shape[0]
    per_owner = angles // rows
    lines = per_owner * slices
    factor = 1.0 / math.sqrt(slab_rows * rows)
    f32 = lambda count: jax.ShapeDtypeStruct((count, lanes), jnp.float32)
    angle = lax.axis_index("row") * per_owner + lax.axis_index("col") // slices
    shear = lax.dynamic_index_in_dim(shear_weights, angle, 0, keepdims=False)
    offset = lax.dynamic_slice_in_dim(shear_offsets, angle, 1, 0)

    tilesum = jnp.einsum("ax,sxy->asy", ray_weights, volume, precision=highest)
    received = exchange(tilesum.reshape(angles * slices, lanes), "row")
    packed = pl.pallas_call(
        lambda *refs: to_lines(rows, lines, *refs),
        out_shape=f32(lines * (rows + 1)),
        in_specs=[VMEM, VMEM],
        out_specs=VMEM,
        name="to_lines",
    )(received, measured.reshape(lines, lanes))
    line = exchange(packed, "col")
    answer = pl.pallas_call(
        lambda *refs: middle(rows, cols, factor, *refs),
        out_shape=f32(cols * (rows + 1)),
        in_specs=[SMEM, VMEM, VMEM],
        out_specs=VMEM,
        scratch_shapes=[pltpu.VMEM((2 * cols, lanes), jnp.float32), pltpu.VMEM((2 * cols, lanes), jnp.float32)],
        name="middle",
    )(offset, line, shear)
    returned = exchange(answer, "col")
    tiles, residual = pl.pallas_call(
        lambda *refs: to_tiles(rows, lines, *refs),
        out_shape=(f32(rows * lines), f32(lines)),
        in_specs=[VMEM],
        out_specs=(VMEM, VMEM),
        name="to_tiles",
    )(returned)
    arrived = exchange(tiles, "row").reshape(angles, slices, lanes)
    gradient = jnp.einsum("ax,asy->sxy", ray_weights, arrived, precision=highest) * factor
    return (residual.reshape(measured.shape), gradient)


def solution(mesh):
    placed = (P(None, "row", "col"), P(None, "row"), P(), P(), P("row", None, "col"))
    return jax.shard_map(
        on_device,
        mesh=mesh,
        in_specs=placed,
        out_specs=(P("row", None, "col"), P(None, "row", "col")),
        check_vma=False,
    )
```

time: 217 us -> 107 us (0.49)
  local copies, waits for them, and re-layouts: 66.5 us -> 3.38 us
  blocking collectives: 82.8 us -> 60.4 us
  waiting for transfers between devices: 37.2 us -> 19.2 us
  Pallas kernels: 0 us -> 6.05 us
  starting transfers between devices: 19.4 us -> 13.5 us
  other arithmetic: 5.45 us -> 0 us
    gather x6 -> x0, local copies, waits for them, and re-layouts: 49 us -> none  [rotate_cols(): reordered = jnp.take_along_axis(spread_out, source[:, :, None], axis=1)]
    all_to_all x4 -> x3, blocking collectives: 82.8 us -> 60.4 us  [exchange(): lax.all_to_all(values.reshape(rows, 1, lanes), axis, 0, 0, tiled=True)]
    all_to_all x2 -> x1, waiting for transfers between devices: 37.2 us -> 19.2 us  [exchange(): lax.all_to_all(values.reshape(rows, 1, lanes), axis, 0, 0, tiled=True)]
    all_to_all x5 -> x0, local copies, waits for them, and re-layouts: 6.52 us -> none  [the longest x3 4.34 us: rotate_cols(): lax.all_to_all(pieces, 'col', split_axis=1, concat_axis=1, tiled=True)]
    unnamed x19 -> x9, local copies, waits for them, and re-layouts: 8.32 us -> 2.03 us
    pallas_call x0 -> x3, Pallas kernels: none -> 6.05 us  [the longest x1 2.69 us: on_device(): pl.pallas_call(lambda *refs: middle(rows, cols, factor, *refs), out_shape...]
    all_to_all x2 -> x1, starting transfers between devices: 19.4 us -> 13.5 us  [exchange(): lax.all_to_all(values.reshape(rows, 1, lanes), axis, 0, 0, tiled=True)]
    all_to_all x4 -> x0, other arithmetic: 4.95 us -> none  [the longest x2 2.49 us: rotate_cols(): lax.all_to_all(pieces, 'col', split_axis=1, concat_axis=1, tiled=True)]
  transfers between devices with their start and end apart: 2 -> 1, of which waited for: 2 -> 1; matrix products, arithmetic and copies ran while one was open for 0% -> 1% of each run, Pallas kernels for 0% -> 0%
where the time goes in v1:
time: 107 us; the launch traced here: 106 us
  blocking collectives  60.4 us (56%)
  waiting for transfers between devices  19.2 us (18%)
  starting transfers between devices  13.5 us (13%)
  Pallas kernels  6.05 us (6%)
  local copies, waits for them, and re-layouts  3.38 us (3%)
  matrix products  3.18 us (3%)
    all_to_all x3, blocking collectives, exchange(): lax.all_to_all(values.reshape(rows, 1, lanes), axis, 0, 0, tiled=True)  60.4 us
    all_to_all x1, waiting for transfers between devices, exchange(): lax.all_to_all(values.reshape(rows, 1, lanes), axis, 0, 0, tiled=True)  19.2 us
    all_to_all x1, starting transfers between devices, exchange(): lax.all_to_all(values.reshape(rows, 1, lanes), axis, 0, 0, tiled=True)  13.5 us
    pallas_call x1, Pallas kernels, on_device(): pl.pallas_call(lambda *refs: middle(rows, cols, factor, *refs), out_shape...  2.69 us
    dot_general x1, matrix products, on_device(): tilesum = jnp.einsum('ax,sxy->asy', ray_weights, volume, precision=highest)  2.16 us
  transfers between devices with their start and end apart: 1, of which 1 were waited for; matrix products, arithmetic and copies ran while one was open for 1% of the time, Pallas kernels for 0%

profile of v1, /device:TPU:1, one launch (start us, length us, event | category | flops | bytes accessed | tf_op | source)
XLA Modules:
  0.0 106.4 jit_solution(4977463792911717154)
XLA Ops:
  0.6 0.0 copy-start
  0.6 0.0 copy-start.3
  0.7 2.2 %fusion.3 = f32[64,8,128]{2,0,1:T(8,128)S(1)} fusion(f32[8,256,128]{2,1,0:T(8,128)} %param.5, f32[64,256]{1,0:T(8,128)} %param.6), kind=kOutput, calls=%fused_computation.4 | convolution fusion | flops 201326592 | bytes 1376256 | tf_op jit(solution)/shard_map/ax,sxy->asy/dot_general | solution.py:72
  2.8 0.0 copy-start.2
  2.8 0.2 copy.14
  3.0 18.7 %all_to_all.20 = f32[512,1,128]{2,1,0:T(1,128)} all-to-all(f32[512,1,128]{2,1,0:T(1,128)S(1)} %bitcast.32), channel_id=1, replica_groups=mesh['row'=16,'col'=32] {'row'}, dimensions={0} | all-to-all | bytes 524288 | tf_op jit(solution)/shard_map/all_to_all | solution.py:55
  21.7 1.7 %to_lines.1 = f32[544,128]{1,0:T(8,128)} custom-call(f32[512,128]{1,0:T(8,128)} %bitcast.33, f32[32,128]{1,0:T(8,128)} %bitcast.36), custom_call_target="tpu_custom_call" | custom-call | tf_op jit(solution)/shard_map/to_lines/pallas_call | solution.py:74
  23.4 13.5 %all-to-all-start.1 = ((f32[544,1,128]{2,1,0:T(1,128)}), f32[544,1,128]{2,1,0:T(1,128)S(1)}, u32[]{:S(2)}, u32[]{:S(2)}) async-start(f32[544,1,128]{2,1,0:T(1,128)} %bitcast.28), calls=%async_computation.1 | async-start | bytes 557056 | tf_op jit(solution)/shard_map/all_to_all | solution.py:55
  36.9 0.0 copy-done.3
  37.0 0.6 dynamic_slice.7.refs_0_
  37.5 0.0 copy-done
  37.5 0.6 dynamic-slice_bitcast_fusion.refs_2_
  38.1 19.2 %all-to-all-done.1 = f32[544,1,128]{2,1,0:T(1,128)S(1)} async-done(((f32[544,1,128]{2,1,0:T(1,128)}), f32[544,1,128]{2,1,0:T(1,128)S(1)}, u32[]{:S(2)}, u32[]{:S(2)}) %all-to-all-start.1) | async-done | bytes 278560 | tf_op jit(solution)/shard_map/all_to_all | solution.py:55
  57.3 0.0 copy-start.1
  57.3 0.7 copy-done.1
  58.0 2.7 %middle.1 = f32[544,128]{1,0:T(8,128)} custom-call(s32[1]{0:T(128)} %dynamic_slice.7.refs_0_, f32[544,128]{1,0:T(8,128)} %bitcast.30, bf16[128,128]{1,0:T(8,128)(2,1)} %dynamic-slice_bitcast_fusion.refs_2_), custom_call_target="tpu_custom_call" | custom-call | tf_op jit(solution)/shard_map/middle/pallas_call | solution.py:82
  60.7 23.7 %all_to_all.21 = f32[544,1,128]{2,1,0:T(1,128)} all-to-all(f32[544,1,128]{2,1,0:T(1,128)} %bitcast.31), channel_id=1, replica_groups=mesh['row'=16,'col'=32] {'col'}, dimensions={0} | all-to-all | bytes 557056 | tf_op jit(solution)/shard_map/all_to_all | solution.py:55
  84.4 1.7 %to_tiles.1 = (f32[512,128]{1,0:T(8,128)}, f32[32,128]{1,0:T(8,128)}) custom-call(f32[544,128]{1,0:T(8,128)} %bitcast.29), custom_call_target="tpu_custom_call" | custom-call | tf_op jit(solution)/shard_map/to_tiles/pallas_call | solution.py:91
  86.0 18.0 %all_to_all.22 = f32[512,1,128]{2,1,0:T(1,128)S(1)} all-to-all(f32[512,1,128]{2,1,0:T(1,128)} %bitcast.35), channel_id=1, replica_groups=mesh['row'=16,'col'=32] {'row'}, dimensions={0} | all-to-all | bytes 524288 | tf_op jit(solution)/shard_map/all_to_all | solution.py:55
  104.1 0.0 copy-done.2
  104.1 1.0 fusion
  105.1 1.3 %copy.20 = f32[8,256,128]{2,1,0:T(8,128)} copy(f32[8,256,128]{1,2,0:T(8,128)S(1)} %fusion) | data formatting | bytes 2097152
Async XLA Ops:
  0.6 36.9 %copy-start = (bf16[64,128,128]{2,1,0:T(8,128)(2,1)S(1)}, bf16[64,128,128]{2,1,0:T(8,128)(2,1)}, u32[]{:S(2)}) copy-start(bf16[64,128,128]{2,1,0:T(8,128)(2,1)} %param.7) | copy-start | bytes 6291460
  0.6 36.3 %copy-start.3 = (s32[64]{0:T(128)S(1)}, s32[64]{0:T(128)}, u32[]{:S(2)}) copy-start(s32[64]{0:T(128)} %param.8) | copy-start | bytes 772
  2.8 101.3 %copy-start.2 = (f32[64,256]{1,0:T(8,128)S(1)}, f32[64,256]{1,0:T(8,128)}, u32[]{:S(2)}) copy-start(f32[64,256]{1,0:T(8,128)} %param.6) | copy-start | bytes 196612
  23.4 33.9 %all-to-all-start.1 = ((f32[544,1,128]{2,1,0:T(1,128)}), f32[544,1,128]{2,1,0:T(1,128)S(1)}, u32[]{:S(2)}, u32[]{:S(2)}) async-start(f32[544,1,128]{2,1,0:T(1,128)} %bitcast.28), calls=%async_computation.1 | async-start | bytes 557056 | tf_op jit(solution)/shard_map/all_to_all | solution.py:55
  57.3 0.7 copy-start.1

commit v2 on v1

v2 whole, which is shorter than its diff:
```python
import math

import jax
import jax.numpy as jnp
from jax import lax
from jax.experimental import pallas as pl
from jax.experimental.pallas import tpu as pltpu
from jax.sharding import PartitionSpec as P

ANY = pl.BlockSpec(memory_space=pl.ANY)
VMEM = pl.BlockSpec(memory_space=pltpu.VMEM)
SMEM = pl.BlockSpec(memory_space=pltpu.SMEM)


def split(values):
    high = values.astype(jnp.bfloat16)
    return high, (values - high.astype(jnp.float32)).astype(jnp.bfloat16)


def dot(left, right, contract):
    return lax.dot_general(left, right, ((contract[:1], contract[1:]), ((), ())), preferred_element_type=jnp.float32)


def sums(volume_ref, weights_ref, shear_ref, tiles_ref, owned_ref, slab_ref, rays_ref, slab_sems, rays_sem, shear_sem, *, angle_of):
    slices, _, lanes = slab_ref.shape
    angles = rays_ref.shape[0]
    rays_copy = pltpu.make_async_copy(weights_ref, rays_ref, rays_sem)
    rays_copy.start()
    copies = [
        pltpu.make_async_copy(volume_ref.at[pl.ds(s, 2)], slab_ref.at[pl.ds(s, 2)], slab_sems.at[s // 2])
        for s in range(0, slices, 2)
    ]
    for copy in copies:
        copy.start()
    shear_copy = pltpu.make_async_copy(shear_ref.at[angle_of()], owned_ref, shear_sem)
    shear_copy.start()
    rays_copy.wait()
    rays_high, rays_low = split(rays_ref[...])
    rays_both = jnp.concatenate([rays_high, rays_low], axis=0)
    for s in range(0, slices, 2):
        copies[s // 2].wait()
        high, low = split(jnp.concatenate([slab_ref[s], slab_ref[s + 1]], axis=1))
        both = dot(rays_both, high, (1, 0))
        tiles = both[:angles] + both[angles:] + dot(rays_high, low, (1, 0))
        tiles_ref[pl.ds(s, angles, stride=slices), :] = tiles[:, :lanes]
        tiles_ref[pl.ds(s + 1, angles, stride=slices), :] = tiles[:, lanes:]
    shear_copy.wait()


def to_lines(tiles_ref, extra_ref, out_ref):
    lines = extra_ref.shape[0]
    rows = tiles_ref.shape[0] // lines
    for r in range(rows):
        out_ref[pl.ds(r, lines, stride=rows + 1), :] = tiles_ref[r * lines : (r + 1) * lines, :]
    out_ref[pl.ds(rows, lines, stride=rows + 1), :] = extra_ref[...]


def to_tiles(in_ref, tiles_ref, extra_ref):
    lines = extra_ref.shape[0]
    rows = tiles_ref.shape[0] // lines
    for r in range(rows):
        tiles_ref[r * lines : (r + 1) * lines, :] = in_ref[pl.ds(r, lines, stride=rows + 1), :]
    extra_ref[...] = in_ref[pl.ds(rows, lines, stride=rows + 1), :]


def middle(offset_ref, in_ref, shear_ref, out_ref, sum_ref, twice_ref, *, rows, cols, factor, angle_of):
    offset = offset_ref[angle_of()]
    sum_ref[...] = jnp.zeros_like(sum_ref)
    for r in range(rows):
        window = pl.ds(lax.rem(offset * r, cols), cols)
        sum_ref[window, :] = sum_ref[window, :] + in_ref[pl.ds(r, cols, stride=rows + 1), :]
    total = (sum_ref[:cols, :] + sum_ref[cols:, :]) * factor
    shear = shear_ref[...]
    both = dot(jnp.concatenate(split(total), axis=0), shear, (1, 0))
    residual = both[:cols] + both[cols:] - in_ref[pl.ds(rows, cols, stride=rows + 1), :]
    both = dot(jnp.concatenate(split(residual), axis=0), shear, (1, 1))
    returning = both[:cols] + both[cols:]
    twice_ref[:cols, :] = returning
    twice_ref[cols:, :] = returning
    for r in range(rows):
        out_ref[pl.ds(r, cols, stride=rows + 1), :] = twice_ref[pl.ds(lax.rem(offset * r, cols), cols), :]
    out_ref[pl.ds(rows, cols, stride=rows + 1), :] = residual


def spread_back(tiles_ref, rays_ref, residual_ref, out_ref, residual_out_ref, slab_ref, sems, residual_sem, *, factor):
    slices, _, lanes = slab_ref.shape
    angles = rays_ref.shape[0]
    residual_copy = pltpu.make_async_copy(residual_ref, residual_out_ref, residual_sem)
    residual_copy.start()
    rays = rays_ref[...] * factor
    high = rays.astype(jnp.bfloat16).astype(jnp.float32)
    rays = jnp.concatenate([high, high, rays - high], axis=0).T.astype(jnp.bfloat16)
    copies = []
    for s in range(0, slices, 2):
        pair = [tiles_ref[pl.ds(t, angles, stride=slices), :] for t in (s, s + 1)]
        high, low = split(jnp.concatenate(pair, axis=1))
        slab = dot(rays, jnp.concatenate([high, low, high], axis=0), (1, 0))
        slab_ref[s] = slab[:, :lanes]
        slab_ref[s + 1] = slab[:, lanes:]
        copy = pltpu.make_async_copy(slab_ref.at[pl.ds(s, 2)], out_ref.at[pl.ds(s, 2)], sems.at[s // 2])
        copy.start()
        copies.append(copy)
    for copy in copies:
        copy.wait()
    residual_copy.wait()


def exchange(values, axis):
    rows, lanes = values.shape
    return lax.all_to_all(values.reshape(rows, 1, lanes), axis, 0, 0, tiled=True).reshape(rows, lanes)


def near(values):
    return pltpu.with_memory_space_constraint(values, pltpu.VMEM)


def on_device(volume, ray_weights, shear_weights, shear_offsets, measured):
    rows = lax.axis_size("row")
    cols = lax.axis_size("col")
    slices, slab_rows, lanes = volume.shape
    angles = ray_weights.shape[0]
    per_owner = angles // rows
    lines = per_owner * slices
    factor = 1.0 / math.sqrt(slab_rows * rows)
    f32 = jnp.float32
    on_chip = lambda count: pltpu.VMEM((count, lanes), f32)
    angle_of = lambda: lax.axis_index("row") * per_owner + lax.axis_index("col") // slices

    tilesum, shear = pl.pallas_call(
        lambda *refs: sums(*refs, angle_of=angle_of),
        out_shape=(on_chip(angles * slices), pltpu.VMEM(shear_weights.shape[1:], shear_weights.dtype)),
        in_specs=[ANY, ANY, ANY],
        out_specs=(VMEM, VMEM),
        scratch_shapes=[
            pltpu.VMEM(volume.shape, f32),
            pltpu.VMEM(ray_weights.shape, f32),
            pltpu.SemaphoreType.DMA((slices // 2,)),
            pltpu.SemaphoreType.DMA,
            pltpu.SemaphoreType.DMA,
        ],
        name="sums",
    )(volume, ray_weights, shear_weights)
    received = exchange(tilesum, "row")
    packed = pl.pallas_call(
        to_lines,
        out_shape=on_chip(lines * (rows + 1)),
        in_specs=[VMEM, VMEM],
        out_specs=VMEM,
        name="to_lines",
    )(near(received), near(measured.reshape(lines, lanes)))
    line = exchange(packed, "col")
    answer = pl.pallas_call(
        lambda *refs: middle(*refs, rows=rows, cols=cols, factor=factor, angle_of=angle_of),
        out_shape=on_chip(cols * (rows + 1)),
        in_specs=[SMEM, VMEM, VMEM],
        out_specs=VMEM,
        scratch_shapes=[on_chip(2 * cols), on_chip(2 * cols)],
        name="middle",
    )(pltpu.with_memory_space_constraint(shear_offsets, pltpu.SMEM), near(line), near(shear))
    returned = exchange(answer, "col")
    tiles, residual = pl.pallas_call(
        to_tiles,
        out_shape=(on_chip(rows * lines), on_chip(lines)),
        in_specs=[VMEM],
        out_specs=(VMEM, VMEM),
        name="to_tiles",
    )(near(returned))
    arrived = exchange(tiles, "row")
    gradient, residual = pl.pallas_call(
        lambda *refs: spread_back(*refs, factor=factor),
        out_shape=(jax.ShapeDtypeStruct(volume.shape, f32), jax.ShapeDtypeStruct(residual.shape, f32)),
        in_specs=[VMEM, VMEM, VMEM],
        out_specs=(ANY, ANY),
        scratch_shapes=[
            pltpu.VMEM(volume.shape, f32),
            pltpu.SemaphoreType.DMA((slices // 2,)),
            pltpu.SemaphoreType.DMA,
        ],
        name="spread_back",
    )(near(arrived), near(ray_weights), near(residual))
    return (residual.reshape(measured.shape), gradient)


def solution(mesh):
    placed = (P(None, "row", "col"), P(None, "row"), P(), P(), P("row", None, "col"))
    return jax.shard_map(
        on_device,
        mesh=mesh,
        in_specs=placed,
        out_specs=(P("row", None, "col"), P(None, "row", "col")),
        check_vma=False,
    )
```

time: 107 us -> 98.5 us (0.921)
  blocking collectives: 60.4 us -> 93.1 us
  waiting for transfers between devices: 19.2 us -> 0 us
  starting transfers between devices: 13.5 us -> 0 us
  local copies, waits for them, and re-layouts: 3.38 us -> 0.01 us
  matrix products: 3.18 us -> 0 us
  Pallas kernels: 6.05 us -> 4.34 us
    all_to_all x3 -> x4, blocking collectives: 60.4 us -> 93.1 us  [exchange(): lax.all_to_all(values.reshape(rows, 1, lanes), axis, 0, 0, tiled=True)]
    all_to_all x1 -> x0, waiting for transfers between devices: 19.2 us -> none  [exchange(): lax.all_to_all(values.reshape(rows, 1, lanes), axis, 0, 0, tiled=True)]
    all_to_all x1 -> x0, starting transfers between devices: 13.5 us -> none  [exchange(): lax.all_to_all(values.reshape(rows, 1, lanes), axis, 0, 0, tiled=True)]
    dot_general x2 -> x0, matrix products: 3.18 us -> none  [the longest x1 2.16 us: on_device(): tilesum = jnp.einsum('ax,sxy->asy', ray_weights, volume, precision=highest)]
    unnamed x9 -> x4, local copies, waits for them, and re-layouts: 2.03 us -> 0.01 us
    pallas_call x3 -> x5, Pallas kernels: 6.05 us -> 4.34 us  [the longest x1 1.95 us: on_device(): pl.pallas_call(lambda *refs: sums(*refs, angle_of=angle_of), out_shape=(o...]
  transfers between devices with their start and end apart: 1 -> 0, of which waited for: 1 -> 0; matrix products, arithmetic and copies ran while one was open for 1% -> 0% of each run, Pallas kernels for 0% -> 0%
where the time goes in v2:
time: 98.5 us; the launch traced here: 98.2 us
  blocking collectives  93.1 us (95%)
  Pallas kernels  4.34 us (4%)
    all_to_all x4, blocking collectives, exchange(): lax.all_to_all(values.reshape(rows, 1, lanes), axis, 0, 0, tiled=True)  93.1 us

profile of v2, /device:TPU:1, one launch (start us, length us, event | category | flops | bytes accessed | tf_op | source)
XLA Modules:
  0.0 98.2 jit_solution(7228855158922745462)
XLA Ops:
  0.6 0.0 copy-start.1
  0.6 2.0 %sums.1 = (f32[512,128]{1,0:T(8,128)S(1)}, bf16[128,128]{1,0:T(8,128)(2,1)S(1)}) custom-call(f32[8,256,128]{2,1,0:T(8,128)} %refs_0_.2, f32[64,256]{1,0:T(8,128)} %refs_1_.3, bf16[64,128,128]{2,1,0:T(8,128)(2,1)} %refs_2_.1), custom_call_target="tpu_custom_call" | custom-call | tf_op jit(solution)/shard_map/sums/pallas_call | solution.py:129
  2.6 0.0 copy-start
  2.6 18.2 %all_to_all.20 = f32[512,1,128]{2,1,0:T(1,128)S(1)} all-to-all(f32[512,1,128]{2,1,0:T(1,128)S(1)} %bitcast.25), channel_id=1, replica_groups=mesh['row'=16,'col'=32] {'row'}, dimensions={0} | all-to-all | bytes 524288 | tf_op jit(solution)/shard_map/all_to_all | solution.py:110
  20.8 0.0 copy-done.1
  20.8 34.3 %all_to_all.21 = f32[544,1,128]{2,1,0:T(1,128)S(1)} all-to-all(f32[544,1,128]{2,1,0:T(1,128)S(1)} %bitcast.19), channel_id=1, replica_groups=mesh['row'=16,'col'=32] {'col'}, dimensions={0} | all-to-all | bytes 557056 | tf_op jit(solution)/shard_map/all_to_all | solution.py:110
  55.1 1.1 %middle.1 = f32[544,128]{1,0:T(8,128)S(1)} custom-call(s32[64]{0:T(128)} %refs_0_.3, f32[544,128]{1,0:T(8,128)S(1)} %bitcast.20, bf16[128,128]{1,0:T(8,128)(2,1)S(1)} %get-tuple-element.9.refs_2_), custom_call_target="tpu_custom_call" | custom-call | tf_op jit(solution)/shard_map/middle/pallas_call | solution.py:152
  56.2 24.7 %all_to_all.22 = f32[544,1,128]{2,1,0:T(1,128)S(1)} all-to-all(f32[544,1,128]{2,1,0:T(1,128)S(1)} %bitcast.21), channel_id=1, replica_groups=mesh['row'=16,'col'=32] {'col'}, dimensions={0} | all-to-all | bytes 557056 | tf_op jit(solution)/shard_map/all_to_all | solution.py:110
  80.8 16.0 %all_to_all.23 = f32[512,1,128]{2,1,0:T(1,128)S(1)} all-to-all(f32[512,1,128]{2,1,0:T(1,128)S(1)} %bitcast.24), channel_id=1, replica_groups=mesh['row'=16,'col'=32] {'row'}, dimensions={0} | all-to-all | bytes 524288 | tf_op jit(solution)/shard_map/all_to_all | solution.py:110
  96.9 0.0 copy-done
  96.9 1.3 %spread_back.1 = (f32[8,256,128]{2,1,0:T(8,128)}, f32[32,128]{1,0:T(8,128)}) custom-call(f32[512,128]{1,0:T(8,128)S(1)} %bitcast.22, f32[64,256]{1,0:T(8,128)S(1)} %copy-done, f32[32,128]{1,0:T(8,128)S(1)} %get-tuple-element.11.refs_2_), custom_call_target="tpu_custom_call" | custom-call | tf_op jit(solution)/shard_map/spread_back/pallas_call | solution.py:169
  (2 shorter events, 0.0 us)
Async XLA Ops:
  0.6 20.2 %copy-start.1 = (f32[4,8,128]{2,1,0:T(8,128)S(1)}, f32[4,8,128]{2,1,0:T(8,128)}, u32[]{:S(2)}) copy-start(f32[4,8,128]{2,1,0:T(8,128)} %param.9) | copy-start | bytes 49156
  2.6 94.3 %copy-start = (f32[64,256]{1,0:T(8,128)S(1)}, f32[64,256]{1,0:T(8,128)}, u32[]{:S(2)}) copy-start(f32[64,256]{1,0:T(8,128)} %refs_1_.3) | copy-start | bytes 196612

commit v3 on v2

--- a/solution.py
+++ b/solution.py
@@ -9,7 +9,6 @@
 
 ANY = pl.BlockSpec(memory_space=pl.ANY)
 VMEM = pl.BlockSpec(memory_space=pltpu.VMEM)
-SMEM = pl.BlockSpec(memory_space=pltpu.SMEM)
 
 
 def split(values):
@@ -21,29 +20,32 @@
     return lax.dot_general(left, right, ((contract[:1], contract[1:]), ((), ())), preferred_element_type=jnp.float32)
 
 
-def sums(volume_ref, weights_ref, shear_ref, tiles_ref, owned_ref, slab_ref, rays_ref, slab_sems, rays_sem, shear_sem, *, angle_of):
+def sums(volume_ref, weights_ref, shear_ref, offsets_ref, tiles_ref, owned_ref, offset_ref, slab_ref, rays_ref, table_ref, slab_sems, rays_sem, shear_sem, table_sem, *, angle_of):
     slices, _, lanes = slab_ref.shape
     angles = rays_ref.shape[0]
+    half = slices // 2
+    angle = angle_of()
     rays_copy = pltpu.make_async_copy(weights_ref, rays_ref, rays_sem)
-    rays_copy.start()
-    copies = [
-        pltpu.make_async_copy(volume_ref.at[pl.ds(s, 2)], slab_ref.at[pl.ds(s, 2)], slab_sems.at[s // 2])
-        for s in range(0, slices, 2)
+    slab_copies = [
+        pltpu.make_async_copy(volume_ref.at[pl.ds(s, half)], slab_ref.at[pl.ds(s, half)], slab_sems.at[s // half])
+        for s in range(0, slices, half)
     ]
-    for copy in copies:
+    shear_copy = pltpu.make_async_copy(shear_ref.at[angle], owned_ref, shear_sem)
+    table_copy = pltpu.make_async_copy(offsets_ref, table_ref, table_sem)
+    for copy in (rays_copy, *slab_copies, shear_copy, table_copy):
         copy.start()
-    shear_copy = pltpu.make_async_copy(shear_ref.at[angle_of()], owned_ref, shear_sem)
-    shear_copy.start()
     rays_copy.wait()
     rays_high, rays_low = split(rays_ref[...])
     rays_both = jnp.concatenate([rays_high, rays_low], axis=0)
-    for s in range(0, slices, 2):
-        copies[s // 2].wait()
-        high, low = split(jnp.concatenate([slab_ref[s], slab_ref[s + 1]], axis=1))
+    for s in range(0, slices, half):
+        slab_copies[s // half].wait()
+        high, low = split(jnp.concatenate([slab_ref[s + t] for t in range(half)], axis=1))
         both = dot(rays_both, high, (1, 0))
         tiles = both[:angles] + both[angles:] + dot(rays_high, low, (1, 0))
-        tiles_ref[pl.ds(s, angles, stride=slices), :] = tiles[:, :lanes]
-        tiles_ref[pl.ds(s + 1, angles, stride=slices), :] = tiles[:, lanes:]
+        for t in range(half):
+            tiles_ref[pl.ds(s + t, angles, stride=slices), :] = tiles[:, t * lanes : (t + 1) * lanes]
+    table_copy.wait()
+    offset_ref[...] = jnp.full(offset_ref.shape, table_ref[angle], offset_ref.dtype)
     shear_copy.wait()
 
 
@@ -63,8 +65,8 @@
     extra_ref[...] = in_ref[pl.ds(rows, lines, stride=rows + 1), :]
 
 
-def middle(offset_ref, in_ref, shear_ref, out_ref, sum_ref, twice_ref, *, rows, cols, factor, angle_of):
-    offset = offset_ref[angle_of()]
+def middle(offset_ref, in_ref, shear_ref, out_ref, sum_ref, twice_ref, *, rows, cols, factor):
+    offset = offset_ref[0, 0]
     sum_ref[...] = jnp.zeros_like(sum_ref)
     for r in range(rows):
         window = pl.ds(lax.rem(offset * r, cols), cols)
@@ -126,20 +128,26 @@
     on_chip = lambda count: pltpu.VMEM((count, lanes), f32)
     angle_of = lambda: lax.axis_index("row") * per_owner + lax.axis_index("col") // slices
 
-    tilesum, shear = pl.pallas_call(
+    tilesum, shear, offset = pl.pallas_call(
         lambda *refs: sums(*refs, angle_of=angle_of),
-        out_shape=(on_chip(angles * slices), pltpu.VMEM(shear_weights.shape[1:], shear_weights.dtype)),
-        in_specs=[ANY, ANY, ANY],
-        out_specs=(VMEM, VMEM),
+        out_shape=(
+            on_chip(angles * slices),
+            pltpu.VMEM(shear_weights.shape[1:], shear_weights.dtype),
+            pltpu.VMEM((8, lanes), shear_offsets.dtype),
+        ),
+        in_specs=[ANY, ANY, ANY, ANY],
+        out_specs=(VMEM, VMEM, VMEM),
         scratch_shapes=[
             pltpu.VMEM(volume.shape, f32),
             pltpu.VMEM(ray_weights.shape, f32),
-            pltpu.SemaphoreType.DMA((slices // 2,)),
+            pltpu.SMEM(shear_offsets.shape, shear_offsets.dtype),
+            pltpu.SemaphoreType.DMA((2,)),
+            pltpu.SemaphoreType.DMA,
             pltpu.SemaphoreType.DMA,
             pltpu.SemaphoreType.DMA,
         ],
         name="sums",
-    )(volume, ray_weights, shear_weights)
+    )(volume, ray_weights, shear_weights, shear_offsets)
     received = exchange(tilesum, "row")
     packed = pl.pallas_call(
         to_lines,
@@ -150,13 +158,13 @@
     )(near(received), near(measured.reshape(lines, lanes)))
     line = exchange(packed, "col")
     answer = pl.pallas_call(
-        lambda *refs: middle(*refs, rows=rows, cols=cols, factor=factor, angle_of=angle_of),
+        lambda *refs: middle(*refs, rows=rows, cols=cols, factor=factor),
         out_shape=on_chip(cols * (rows + 1)),
-        in_specs=[SMEM, VMEM, VMEM],
+        in_specs=[VMEM, VMEM, VMEM],
         out_specs=VMEM,
         scratch_shapes=[on_chip(2 * cols), on_chip(2 * cols)],
         name="middle",
-    )(pltpu.with_memory_space_constraint(shear_offsets, pltpu.SMEM), near(line), near(shear))
+    )(near(offset), near(line), near(shear))
     returned = exchange(answer, "col")
     tiles, residual = pl.pallas_call(
         to_tiles,

time: 98.5 us -> 97.4 us (0.989)
  Pallas kernels: 4.34 us -> 3.3 us
where the time goes in v3:
time: 97.4 us; the launch traced here: 97.1 us
  blocking collectives  93.1 us (96%)
  Pallas kernels  3.3 us (3%)
    all_to_all x4, blocking collectives, exchange(): lax.all_to_all(values.reshape(rows, 1, lanes), axis, 0, 0, tiled=True)  93.1 us

profile of v3, /device:TPU:1, one launch (start us, length us, event | category | flops | bytes accessed | tf_op | source)
XLA Modules:
  0.0 97.1 jit_solution(16294694131198771629)
XLA Ops:
  0.6 0.0 copy-start.1
  0.6 1.6 %sums.1 = (f32[512,128]{1,0:T(8,128)S(1)}, bf16[128,128]{1,0:T(8,128)(2,1)S(1)}, s32[8,128]{1,0:T(8,128)S(1)}) custom-call(f32[8,256,128]{2,1,0:T(8,128)} %refs_0_.1, f32[64,256]{1,0:T(8,128)} %refs_1_.3, bf16[64,128,128]{2,1,0:T(8,128)(2,1)} %refs_2_.1, s32[64]{0:T(128)} %refs_3_.1), custom_call_target="tpu_custom_call" | custom-call | tf_op jit(solution)/shard_map/sums/pallas_call | solution.py:131
  2.2 0.0 copy-start
  2.2 18.2 %all_to_all.20 = f32[512,1,128]{2,1,0:T(1,128)S(1)} all-to-all(f32[512,1,128]{2,1,0:T(1,128)S(1)} %bitcast.24), channel_id=1, replica_groups=mesh['row'=16,'col'=32] {'row'}, dimensions={0} | all-to-all | bytes 524288 | tf_op jit(solution)/shard_map/all_to_all | solution.py:112
  20.4 0.0 copy-done.1
  20.4 34.3 %all_to_all.21 = f32[544,1,128]{2,1,0:T(1,128)S(1)} all-to-all(f32[544,1,128]{2,1,0:T(1,128)S(1)} %bitcast.21), channel_id=1, replica_groups=mesh['row'=16,'col'=32] {'col'}, dimensions={0} | all-to-all | bytes 557056 | tf_op jit(solution)/shard_map/all_to_all | solution.py:112
  54.7 0.4 middle.1
  55.1 24.7 %all_to_all.22 = f32[544,1,128]{2,1,0:T(1,128)S(1)} all-to-all(f32[544,1,128]{2,1,0:T(1,128)S(1)} %bitcast.19), channel_id=1, replica_groups=mesh['row'=16,'col'=32] {'col'}, dimensions={0} | all-to-all | bytes 557056 | tf_op jit(solution)/shard_map/all_to_all | solution.py:112
  79.8 16.0 %all_to_all.23 = f32[512,1,128]{2,1,0:T(1,128)S(1)} all-to-all(f32[512,1,128]{2,1,0:T(1,128)S(1)} %bitcast.25), channel_id=1, replica_groups=mesh['row'=16,'col'=32] {'row'}, dimensions={0} | all-to-all | bytes 524288 | tf_op jit(solution)/shard_map/all_to_all | solution.py:112
  95.8 0.0 copy-done
  95.8 1.3 %spread_back.1 = (f32[8,256,128]{2,1,0:T(8,128)}, f32[32,128]{1,0:T(8,128)}) custom-call(f32[512,128]{1,0:T(8,128)S(1)} %bitcast.22, f32[64,256]{1,0:T(8,128)S(1)} %copy-done, f32[32,128]{1,0:T(8,128)S(1)} %get-tuple-element.13.refs_2_), custom_call_target="tpu_custom_call" | custom-call | tf_op jit(solution)/shard_map/spread_back/pallas_call | solution.py:177
  (2 shorter events, 0.0 us)
Async XLA Ops:
  0.6 19.8 %copy-start.1 = (f32[4,8,128]{2,1,0:T(8,128)S(1)}, f32[4,8,128]{2,1,0:T(8,128)}, u32[]{:S(2)}) copy-start(f32[4,8,128]{2,1,0:T(8,128)} %param.9) | copy-start | bytes 49156
  2.2 93.6 %copy-start = (f32[64,256]{1,0:T(8,128)S(1)}, f32[64,256]{1,0:T(8,128)}, u32[]{:S(2)}) copy-start(f32[64,256]{1,0:T(8,128)} %refs_1_.3) | copy-start | bytes 196612

commit v4 on v3

v4 whole, which is shorter than its diff:
```python
import math

import jax
import jax.numpy as jnp
from jax import lax
from jax.experimental import pallas as pl
from jax.experimental.pallas import tpu as pltpu
from jax.sharding import Mesh, PartitionSpec as P

NEAR = 4
ANY = pl.BlockSpec(memory_space=pl.ANY)
VMEM = pl.BlockSpec(memory_space=pltpu.VMEM)


def split(values):
    high = values.astype(jnp.bfloat16)
    return high, (values - high.astype(jnp.float32)).astype(jnp.bfloat16)


def dot(left, right, contract):
    return lax.dot_general(left, right, ((contract[:1], contract[1:]), ((), ())), preferred_element_type=jnp.float32)


def sums(volume_ref, weights_ref, shear_ref, offsets_ref, tiles_ref, owned_ref, offset_ref, slab_ref, rays_ref, table_ref, slab_sems, rays_sem, shear_sem, table_sem, *, row_of, angle_of):
    slices, _, lanes = slab_ref.shape
    angles = rays_ref.shape[0]
    owned = owned_ref.shape[0]
    half = slices // 2
    rays_copy = pltpu.make_async_copy(weights_ref, rays_ref, rays_sem)
    slab_copies = [
        pltpu.make_async_copy(volume_ref.at[pl.ds(s, half)], slab_ref.at[pl.ds(s, half)], slab_sems.at[s // half])
        for s in range(0, slices, half)
    ]
    shear_copy = pltpu.make_async_copy(shear_ref.at[pl.ds(row_of() * owned, owned)], owned_ref, shear_sem)
    table_copy = pltpu.make_async_copy(offsets_ref, table_ref, table_sem)
    for copy in (rays_copy, *slab_copies, shear_copy, table_copy):
        copy.start()
    rays_copy.wait()
    rays_high, rays_low = split(rays_ref[...])
    rays_both = jnp.concatenate([rays_high, rays_low], axis=0)
    for s in range(0, slices, half):
        slab_copies[s // half].wait()
        high, low = split(jnp.concatenate([slab_ref[s + t] for t in range(half)], axis=1))
        both = dot(rays_both, high, (1, 0))
        tiles = both[:angles] + both[angles:] + dot(rays_high, low, (1, 0))
        for t in range(half):
            tiles_ref[pl.ds(s + t, angles, stride=slices), :] = tiles[:, t * lanes : (t + 1) * lanes]
    table_copy.wait()
    offset_ref[...] = jnp.full(offset_ref.shape, table_ref[angle_of()], offset_ref.dtype)
    shear_copy.wait()


def push(offset_ref, tiles_ref, line_ref, *, first_of):
    cols = line_ref.shape[0]
    offset = offset_ref[0, 0]
    first = first_of()
    line_ref[...] = jnp.zeros_like(line_ref)
    for t in range(tiles_ref.shape[0]):
        at = lax.rem(first + t % NEAR + offset * (t // NEAR), cols)
        line_ref[at] = line_ref[at] + tiles_ref[t]


def pull(offset_ref, line_ref, tiles_ref, *, first_of):
    cols = line_ref.shape[0]
    offset = offset_ref[0, 0]
    first = first_of()
    for t in range(tiles_ref.shape[0]):
        tiles_ref[t] = line_ref[lax.rem(first + t % NEAR + offset * (t // NEAR), cols)]


def middle(parts_ref, shear_ref, measured_ref, copies_ref, residual_ref, *, factor):
    count, slices, _ = parts_ref.shape
    for j in range(NEAR):
        total = parts_ref[j]
        for t in range(j + NEAR, count, NEAR):
            total = total + parts_ref[t]
        shear = shear_ref[j]
        both = dot(jnp.concatenate(split(total * factor), axis=0), shear, (1, 0))
        residual = both[:slices] + both[slices:] - measured_ref[j]
        residual_ref[j] = residual
        both = dot(jnp.concatenate(split(residual), axis=0), shear, (1, 1))
        returning = both[:slices] + both[slices:]
        for t in range(j, count, NEAR):
            copies_ref[t] = returning


def spread_back(tiles_ref, rays_ref, residual_ref, out_ref, residual_out_ref, slab_ref, sems, residual_sem, *, factor):
    slices, _, lanes = slab_ref.shape
    angles = rays_ref.shape[0]
    residual_copy = pltpu.make_async_copy(residual_ref, residual_out_ref, residual_sem)
    residual_copy.start()
    rays = rays_ref[...] * factor
    high = rays.astype(jnp.bfloat16).astype(jnp.float32)
    rays = jnp.concatenate([high, high, rays - high], axis=0).T.astype(jnp.bfloat16)
    copies = []
    for s in range(0, slices, 2):
        pair = [tiles_ref[pl.ds(t, angles, stride=slices), :] for t in (s, s + 1)]
        high, low = split(jnp.concatenate(pair, axis=1))
        slab = dot(rays, jnp.concatenate([high, low, high], axis=0), (1, 0))
        slab_ref[s] = slab[:, :lanes]
        slab_ref[s + 1] = slab[:, lanes:]
        copy = pltpu.make_async_copy(slab_ref.at[pl.ds(s, 2)], out_ref.at[pl.ds(s, 2)], sems.at[s // 2])
        copy.start()
        copies.append(copy)
    for copy in copies:
        copy.wait()
    residual_copy.wait()


def exchange(values, axes):
    return lax.all_to_all(values, axes, 0, 0, tiled=True)


def near(values):
    return pltpu.with_memory_space_constraint(values, pltpu.VMEM)


def on_device(volume, ray_weights, shear_weights, shear_offsets, measured):
    rows = lax.axis_size("row")
    cols = lax.axis_size(("far", "near"))
    slices, slab_rows, lanes = volume.shape
    angles = ray_weights.shape[0]
    factor = 1.0 / math.sqrt(slab_rows * rows)
    f32 = jnp.float32
    tiles_of = lambda count: pltpu.VMEM((count, slices, lanes), f32)
    row_of = lambda: lax.axis_index("row")
    angle_of = lambda: lax.axis_index("row") * NEAR + lax.axis_index("near")
    first_of = lambda: lax.axis_index("far") * NEAR

    tilesum, shear, offset = pl.pallas_call(
        lambda *refs: sums(*refs, row_of=row_of, angle_of=angle_of),
        out_shape=(
            pltpu.VMEM((angles * slices, lanes), f32),
            pltpu.VMEM((NEAR,) + shear_weights.shape[1:], shear_weights.dtype),
            pltpu.VMEM((8, lanes), shear_offsets.dtype),
        ),
        in_specs=[ANY, ANY, ANY, ANY],
        out_specs=(VMEM, VMEM, VMEM),
        scratch_shapes=[
            pltpu.VMEM(volume.shape, f32),
            pltpu.VMEM(ray_weights.shape, f32),
            pltpu.SMEM(shear_offsets.shape, shear_offsets.dtype),
            pltpu.SemaphoreType.DMA((2,)),
            pltpu.SemaphoreType.DMA,
            pltpu.SemaphoreType.DMA,
            pltpu.SemaphoreType.DMA,
        ],
        name="sums",
    )(volume, ray_weights, shear_weights, shear_offsets)
    received = exchange(tilesum.reshape(angles, slices, lanes), ("row", "near"))
    line = pl.pallas_call(
        lambda *refs: push(*refs, first_of=first_of),
        out_shape=tiles_of(cols),
        in_specs=[VMEM, VMEM],
        out_specs=VMEM,
        name="push",
    )(near(offset), near(received))
    parts = exchange(line, ("far", "near"))
    answer, residual = pl.pallas_call(
        lambda *refs: middle(*refs, factor=factor),
        out_shape=(tiles_of(cols), tiles_of(NEAR)),
        in_specs=[VMEM, VMEM, VMEM],
        out_specs=(VMEM, VMEM),
        name="middle",
    )(near(parts), near(shear), near(measured))
    returned = exchange(answer, ("far", "near"))
    tiles = pl.pallas_call(
        lambda *refs: pull(*refs, first_of=first_of),
        out_shape=tiles_of(angles),
        in_specs=[VMEM, VMEM],
        out_specs=VMEM,
        name="pull",
    )(near(offset), near(returned))
    arrived = exchange(tiles, ("row", "near")).reshape(angles * slices, lanes)
    gradient, residual = pl.pallas_call(
        lambda *refs: spread_back(*refs, factor=factor),
        out_shape=(jax.ShapeDtypeStruct(volume.shape, f32), jax.ShapeDtypeStruct(residual.shape, f32)),
        in_specs=[VMEM, VMEM, VMEM],
        out_specs=(ANY, ANY),
        scratch_shapes=[
            pltpu.VMEM(volume.shape, f32),
            pltpu.SemaphoreType.DMA((slices // 2,)),
            pltpu.SemaphoreType.DMA,
        ],
        name="spread_back",
    )(near(arrived), near(ray_weights), near(residual))
    return (residual, gradient)


def solution(mesh):
    rows, cols = mesh.devices.shape
    cut = Mesh(mesh.devices.reshape(rows, cols // NEAR, NEAR), ("row", "far", "near"))
    columns = ("far", "near")
    placed = (P(None, "row", columns), P(None, "row"), P(), P(), P("row", None, columns))
    return jax.shard_map(
        on_device,
        mesh=cut,
        in_specs=placed,
        out_specs=(P("row", None, columns), P(None, "row", columns)),
        check_vma=False,
    )
```

time: 97.4 us -> 89.1 us (0.915)
  blocking collectives: 93.1 us -> 84.4 us
    all_to_all x4, blocking collectives: 93.1 us -> 84.4 us  [exchange(): return lax.all_to_all(values, axes, 0, 0, tiled=True)]
where the time goes in v4:
time: 89.1 us; the launch traced here: 88.8 us
  blocking collectives  84.4 us (95%)
  Pallas kernels  3.7 us (4%)
    all_to_all x4, blocking collectives, exchange(): return lax.all_to_all(values, axes, 0, 0, tiled=True)  84.4 us

profile of v4, /device:TPU:1, one launch (start us, length us, event | category | flops | bytes accessed | tf_op | source)
XLA Modules:
  0.0 88.8 jit_solution(1118346805982323915)
XLA Ops:
  0.6 0.0 copy-start.1
  0.6 1.6 %sums.1 = (f32[512,128]{1,0:T(8,128)S(1)}, bf16[4,128,128]{2,1,0:T(8,128)(2,1)S(1)}, s32[8,128]{1,0:T(8,128)S(1)}) custom-call(f32[8,256,128]{2,1,0:T(8,128)} %refs_0_.1, f32[64,256]{1,0:T(8,128)} %refs_1_.3, bf16[64,128,128]{2,1,0:T(8,128)(2,1)} %refs_2_.2, s32[64]{0:T(128)} %refs_3_.1), custom_call_target="tpu_custom_call" | custom-call | tf_op jit(solution)/shard_map/sums/pallas_call | solution.py:130
  2.2 0.0 copy-start
  2.2 20.3 %all_to_all.20.refs_1_ = f32[64,8,128]{2,1,0:T(8,128)S(1)} all-to-all(f32[64,8,128]{2,1,0:T(8,128)S(1)} %bitcast.3), channel_id=1, replica_groups=mesh['row'=16,'far'=8,'near'=4] {'row','near'}, dimensions={0} | all-to-all | bytes 524288 | tf_op jit(solution)/shard_map/all_to_all | solution.py:111
  22.5 0.3 push.1
  22.7 28.7 %all_to_all.21.refs_0_ = f32[32,8,128]{2,1,0:T(8,128)S(1)} all-to-all(f32[32,8,128]{2,1,0:T(8,128)S(1)} %push.1), channel_id=1, replica_groups=mesh['row'=16,'far'=8,'near'=4] {'far','near'}, dimensions={0} | all-to-all | bytes 262144 | tf_op jit(solution)/shard_map/all_to_all | solution.py:111
  51.4 0.0 copy-done.1
  51.4 0.4 middle.1
  51.8 18.2 %all_to_all.22.refs_1_ = f32[32,8,128]{2,1,0:T(8,128)S(1)} all-to-all(f32[32,8,128]{2,1,0:T(8,128)S(1)} %get-tuple-element.12), channel_id=1, replica_groups=mesh['row'=16,'far'=8,'near'=4] {'far','near'}, dimensions={0} | all-to-all | bytes 262144 | tf_op jit(solution)/shard_map/all_to_all | solution.py:111
  70.0 0.2 pull.1
  70.2 17.4 %all_to_all.23 = f32[64,8,128]{2,1,0:T(8,128)S(1)} all-to-all(f32[64,8,128]{2,1,0:T(8,128)S(1)} %pull.1), channel_id=1, replica_groups=mesh['row'=16,'far'=8,'near'=4] {'row','near'}, dimensions={0} | all-to-all | bytes 524288 | tf_op jit(solution)/shard_map/all_to_all | solution.py:111
  87.5 0.0 copy-done
  87.5 1.3 %spread_back.1 = (f32[8,256,128]{2,1,0:T(8,128)}, f32[4,8,128]{2,1,0:T(8,128)}) custom-call(f32[512,128]{1,0:T(8,128)S(1)} %bitcast.2, f32[64,256]{1,0:T(8,128)S(1)} %copy-done, f32[4,8,128]{2,1,0:T(8,128)S(1)} %get-tuple-element.13.refs_2_), custom_call_target="tpu_custom_call" | custom-call | tf_op jit(solution)/shard_map/spread_back/pallas_call | solution.py:175
Async XLA Ops:
  0.6 50.8 %copy-start.1 = (f32[4,8,128]{2,1,0:T(8,128)S(1)}, f32[4,8,128]{2,1,0:T(8,128)}, u32[]{:S(2)}) copy-start(f32[4,8,128]{2,1,0:T(8,128)} %refs_2_.3) | copy-start | bytes 49156
  2.2 85.3 %copy-start = (f32[64,256]{1,0:T(8,128)S(1)}, f32[64,256]{1,0:T(8,128)}, u32[]{:S(2)}) copy-start(f32[64,256]{1,0:T(8,128)} %refs_1_.3) | copy-start | bytes 196612

commit v5 on v4

--- a/solution.py
+++ b/solution.py
@@ -21,7 +21,7 @@
     return lax.dot_general(left, right, ((contract[:1], contract[1:]), ((), ())), preferred_element_type=jnp.float32)
 
 
-def sums(volume_ref, weights_ref, shear_ref, offsets_ref, tiles_ref, owned_ref, offset_ref, slab_ref, rays_ref, table_ref, slab_sems, rays_sem, shear_sem, table_sem, *, row_of, angle_of):
+def sums(volume_ref, weights_ref, shear_ref, offsets_ref, tiles_ref, owned_ref, offset_ref, across_ref, slab_ref, rays_ref, table_ref, slab_sems, rays_sem, shear_sem, table_sem, *, row_of, angle_of, factor):
     slices, _, lanes = slab_ref.shape
     angles = rays_ref.shape[0]
     owned = owned_ref.shape[0]
@@ -38,6 +38,9 @@
     rays_copy.wait()
     rays_high, rays_low = split(rays_ref[...])
     rays_both = jnp.concatenate([rays_high, rays_low], axis=0)
+    scaled = rays_ref[...] * factor
+    high = scaled.astype(jnp.bfloat16).astype(jnp.float32)
+    across_ref[...] = jnp.concatenate([high, high, scaled - high], axis=0).T.astype(jnp.bfloat16)
     for s in range(0, slices, half):
         slab_copies[s // half].wait()
         high, low = split(jnp.concatenate([slab_ref[s + t] for t in range(half)], axis=1))
@@ -50,53 +53,59 @@
     shear_copy.wait()
 
 
-def push(offset_ref, tiles_ref, line_ref, *, first_of):
+def push(offset_ref, tiles_ref, line_ref, sum_ref, *, first_of):
     cols = line_ref.shape[0]
+    rows = tiles_ref.shape[0] // NEAR
+    room = sum_ref.shape[0] // 2
     offset = offset_ref[0, 0]
     first = first_of()
-    line_ref[...] = jnp.zeros_like(line_ref)
-    for t in range(tiles_ref.shape[0]):
-        at = lax.rem(first + t % NEAR + offset * (t // NEAR), cols)
-        line_ref[at] = line_ref[at] + tiles_ref[t]
-
-
-def pull(offset_ref, line_ref, tiles_ref, *, first_of):
+    sum_ref[...] = jnp.zeros_like(sum_ref)
+    for r in range(rows):
+        window = pl.ds(lax.rem(first + offset * r, cols) + r % 2 * room, NEAR)
+        sum_ref[window] = sum_ref[window] + tiles_ref[r * NEAR : (r + 1) * NEAR]
+    line_ref[...] = sum_ref[:cols] + sum_ref[room : room + cols]
+    line_ref[: room - cols] = line_ref[: room - cols] + (sum_ref[cols:room] + sum_ref[room + cols :])
+
+
+def pull(offset_ref, line_ref, tiles_ref, twice_ref, *, first_of):
     cols = line_ref.shape[0]
+    rows = tiles_ref.shape[0] // NEAR
     offset = offset_ref[0, 0]
     first = first_of()
-    for t in range(tiles_ref.shape[0]):
-        tiles_ref[t] = line_ref[lax.rem(first + t % NEAR + offset * (t // NEAR), cols)]
+    twice_ref[:cols] = line_ref[...]
+    twice_ref[cols:] = line_ref[:NEAR]
+    for r in range(rows):
+        tiles_ref[r * NEAR : (r + 1) * NEAR] = twice_ref[pl.ds(lax.rem(first + offset * r, cols), NEAR)]
 
 
 def middle(parts_ref, shear_ref, measured_ref, copies_ref, residual_ref, *, factor):
     count, slices, _ = parts_ref.shape
+    residuals = []
     for j in range(NEAR):
-        total = parts_ref[j]
-        for t in range(j + NEAR, count, NEAR):
-            total = total + parts_ref[t]
-        shear = shear_ref[j]
-        both = dot(jnp.concatenate(split(total * factor), axis=0), shear, (1, 0))
-        residual = both[:slices] + both[slices:] - measured_ref[j]
-        residual_ref[j] = residual
-        both = dot(jnp.concatenate(split(residual), axis=0), shear, (1, 1))
+        shares = [parts_ref[t] for t in range(j, count, NEAR)]
+        while len(shares) > 1:
+            shares = [sum(shares[t : t + 2]) for t in range(0, len(shares), 2)]
+        both = dot(jnp.concatenate(split(shares[0] * factor), axis=0), shear_ref[j], (1, 0))
+        residuals.append(both[:slices] + both[slices:] - measured_ref[j])
+    for j in range(NEAR):
+        residual_ref[j] = residuals[j]
+        both = dot(jnp.concatenate(split(residuals[j]), axis=0), shear_ref[j], (1, 1))
         returning = both[:slices] + both[slices:]
         for t in range(j, count, NEAR):
             copies_ref[t] = returning
 
 
-def spread_back(tiles_ref, rays_ref, residual_ref, out_ref, residual_out_ref, slab_ref, sems, residual_sem, *, factor):
+def spread_back(tiles_ref, across_ref, residual_ref, out_ref, residual_out_ref, slab_ref, sems, residual_sem):
     slices, _, lanes = slab_ref.shape
-    angles = rays_ref.shape[0]
+    angles = tiles_ref.shape[0] // slices
     residual_copy = pltpu.make_async_copy(residual_ref, residual_out_ref, residual_sem)
     residual_copy.start()
-    rays = rays_ref[...] * factor
-    high = rays.astype(jnp.bfloat16).astype(jnp.float32)
-    rays = jnp.concatenate([high, high, rays - high], axis=0).T.astype(jnp.bfloat16)
+    across = across_ref[...]
     copies = []
     for s in range(0, slices, 2):
         pair = [tiles_ref[pl.ds(t, angles, stride=slices), :] for t in (s, s + 1)]
         high, low = split(jnp.concatenate(pair, axis=1))
-        slab = dot(rays, jnp.concatenate([high, low, high], axis=0), (1, 0))
+        slab = dot(across, jnp.concatenate([high, low, high], axis=0), (1, 0))
         slab_ref[s] = slab[:, :lanes]
         slab_ref[s + 1] = slab[:, lanes:]
         copy = pltpu.make_async_copy(slab_ref.at[pl.ds(s, 2)], out_ref.at[pl.ds(s, 2)], sems.at[s // 2])
@@ -127,15 +136,16 @@
     angle_of = lambda: lax.axis_index("row") * NEAR + lax.axis_index("near")
     first_of = lambda: lax.axis_index("far") * NEAR
 
-    tilesum, shear, offset = pl.pallas_call(
-        lambda *refs: sums(*refs, row_of=row_of, angle_of=angle_of),
+    tilesum, shear, offset, across = pl.pallas_call(
+        lambda *refs: sums(*refs, row_of=row_of, angle_of=angle_of, factor=factor),
         out_shape=(
             pltpu.VMEM((angles * slices, lanes), f32),
             pltpu.VMEM((NEAR,) + shear_weights.shape[1:], shear_weights.dtype),
             pltpu.VMEM((8, lanes), shear_offsets.dtype),
+            pltpu.VMEM((slab_rows, 3 * angles), jnp.bfloat16),
         ),
         in_specs=[ANY, ANY, ANY, ANY],
-        out_specs=(VMEM, VMEM, VMEM),
+        out_specs=(VMEM, VMEM, VMEM, VMEM),
         scratch_shapes=[
             pltpu.VMEM(volume.shape, f32),
             pltpu.VMEM(ray_weights.shape, f32),
@@ -153,6 +163,7 @@
         out_shape=tiles_of(cols),
         in_specs=[VMEM, VMEM],
         out_specs=VMEM,
+        scratch_shapes=[tiles_of(2 * (cols + NEAR))],
         name="push",
     )(near(offset), near(received))
     parts = exchange(line, ("far", "near"))
@@ -169,11 +180,12 @@
         out_shape=tiles_of(angles),
         in_specs=[VMEM, VMEM],
         out_specs=VMEM,
+        scratch_shapes=[tiles_of(cols + NEAR)],
         name="pull",
     )(near(offset), near(returned))
     arrived = exchange(tiles, ("row", "near")).reshape(angles * slices, lanes)
     gradient, residual = pl.pallas_call(
-        lambda *refs: spread_back(*refs, factor=factor),
+        spread_back,
         out_shape=(jax.ShapeDtypeStruct(volume.shape, f32), jax.ShapeDtypeStruct(residual.shape, f32)),
         in_specs=[VMEM, VMEM, VMEM],
         out_specs=(ANY, ANY),
@@ -183,7 +195,7 @@
             pltpu.SemaphoreType.DMA,
         ],
         name="spread_back",
-    )(near(arrived), near(ray_weights), near(residual))
+    )(near(arrived), near(across), near(residual))
     return (residual, gradient)
 
 

time: 89.1 us -> 88.6 us (level)
  no operation moved by 1% of the time
where the time goes in v5:
time: 88.6 us; the launch traced here: 88.3 us
  blocking collectives  84.3 us (95%)
  Pallas kernels  3.35 us (4%)
    all_to_all x4, blocking collectives, exchange(): return lax.all_to_all(values, axes, 0, 0, tiled=True)  84.3 us

profile of v5, /device:TPU:1, one launch (start us, length us, event | category | flops | bytes accessed | tf_op | source)
XLA Modules:
  0.0 88.3 jit_solution(7879544816141515616)
XLA Ops:
  0.6 0.0 copy-start
  0.6 1.6 %sums.1 = (f32[512,128]{1,0:T(8,128)S(1)}, bf16[4,128,128]{2,1,0:T(8,128)(2,1)S(1)}, s32[8,128]{1,0:T(8,128)S(1)}, bf16[256,192]{1,0:T(8,128)(2,1)S(1)}) custom-call(f32[8,256,128]{2,1,0:T(8,128)} %refs_0_.1, f32[64,256]{1,0:T(8,128)} %refs_1_.1, bf16[64,128,128]{2,1,0:T(8,128)(2,1)} %refs_2_.2, s32[64]{0:T(128)} %refs_3_.1), custom_call_target="tpu_custom_call" | custom-call | tf_op jit(solution)/shard_map/sums/pallas_call | solution.py:139
  2.3 20.1 %all_to_all.20.refs_1_ = f32[64,8,128]{2,1,0:T(8,128)S(1)} all-to-all(f32[64,8,128]{2,1,0:T(8,128)S(1)} %bitcast.3), channel_id=1, replica_groups=mesh['row'=16,'far'=8,'near'=4] {'row','near'}, dimensions={0} | all-to-all | bytes 524288 | tf_op jit(solution)/shard_map/all_to_all | solution.py:120
  22.4 0.1 push.1
  22.5 28.7 %all_to_all.21.refs_0_ = f32[32,8,128]{2,1,0:T(8,128)S(1)} all-to-all(f32[32,8,128]{2,1,0:T(8,128)S(1)} %push.1), channel_id=1, replica_groups=mesh['row'=16,'far'=8,'near'=4] {'far','near'}, dimensions={0} | all-to-all | bytes 262144 | tf_op jit(solution)/shard_map/all_to_all | solution.py:120
  51.2 0.0 copy-done
  51.2 0.3 middle.1
  51.5 18.2 %all_to_all.22.refs_1_ = f32[32,8,128]{2,1,0:T(8,128)S(1)} all-to-all(f32[32,8,128]{2,1,0:T(8,128)S(1)} %get-tuple-element.13), channel_id=1, replica_groups=mesh['row'=16,'far'=8,'near'=4] {'far','near'}, dimensions={0} | all-to-all | bytes 262144 | tf_op jit(solution)/shard_map/all_to_all | solution.py:120
  69.6 0.1 pull.1
  69.7 17.4 %all_to_all.23 = f32[64,8,128]{2,1,0:T(8,128)S(1)} all-to-all(f32[64,8,128]{2,1,0:T(8,128)S(1)} %pull.1), channel_id=1, replica_groups=mesh['row'=16,'far'=8,'near'=4] {'row','near'}, dimensions={0} | all-to-all | bytes 524288 | tf_op jit(solution)/shard_map/all_to_all | solution.py:120
  87.1 1.2 %spread_back.1 = (f32[8,256,128]{2,1,0:T(8,128)}, f32[4,8,128]{2,1,0:T(8,128)}) custom-call(f32[512,128]{1,0:T(8,128)S(1)} %bitcast.2, bf16[256,192]{1,0:T(8,128)(2,1)S(1)} %get-tuple-element.14.across_ref, f32[4,8,128]{2,1,0:T(8,128)S(1)} %get-tuple-element.15.residual_ref), custom_call_target="tpu_custom_call" | custom-call | tf_op jit(solution)/shard_map/spread_back/pallas_call | solution.py:187
Async XLA Ops:
  0.6 50.6 %copy-start = (f32[4,8,128]{2,1,0:T(8,128)S(1)}, f32[4,8,128]{2,1,0:T(8,128)}, u32[]{:S(2)}) copy-start(f32[4,8,128]{2,1,0:T(8,128)} %refs_2_.3) | copy-start | bytes 49156

commit v6 on v5

--- a/solution.py
+++ b/solution.py
@@ -12,6 +12,10 @@
 VMEM = pl.BlockSpec(memory_space=pltpu.VMEM)
 
 
+def row_order(rows):
+    return sorted(range(rows), key=lambda r: (r % 2 == 0, -r))
+
+
 def split(values):
     high = values.astype(jnp.bfloat16)
     return high, (values - high.astype(jnp.float32)).astype(jnp.bfloat16)
@@ -21,7 +25,7 @@
     return lax.dot_general(left, right, ((contract[:1], contract[1:]), ((), ())), preferred_element_type=jnp.float32)
 
 
-def sums(volume_ref, weights_ref, shear_ref, offsets_ref, tiles_ref, owned_ref, offset_ref, across_ref, slab_ref, rays_ref, table_ref, slab_sems, rays_sem, shear_sem, table_sem, *, row_of, angle_of, factor):
+def sums(volume_ref, weights_ref, shear_ref, offsets_ref, tiles_ref, owned_ref, offset_ref, across_ref, slab_ref, rays_ref, sorted_ref, table_ref, slab_sems, rays_sem, shear_sem, table_sem, *, row_of, angle_of, factor):
     slices, _, lanes = slab_ref.shape
     angles = rays_ref.shape[0]
     owned = owned_ref.shape[0]
@@ -36,9 +40,12 @@
     for copy in (rays_copy, *slab_copies, shear_copy, table_copy):
         copy.start()
     rays_copy.wait()
-    rays_high, rays_low = split(rays_ref[...])
+    for i, r in enumerate(row_order(angles // NEAR)):
+        sorted_ref[i * NEAR : (i + 1) * NEAR, :] = rays_ref[r * NEAR : (r + 1) * NEAR, :]
+    rays = sorted_ref[...]
+    rays_high, rays_low = split(rays)
     rays_both = jnp.concatenate([rays_high, rays_low], axis=0)
-    scaled = rays_ref[...] * factor
+    scaled = rays * factor
     high = scaled.astype(jnp.bfloat16).astype(jnp.float32)
     across_ref[...] = jnp.concatenate([high, high, scaled - high], axis=0).T.astype(jnp.bfloat16)
     for s in range(0, slices, half):
@@ -60,9 +67,9 @@
     offset = offset_ref[0, 0]
     first = first_of()
     sum_ref[...] = jnp.zeros_like(sum_ref)
-    for r in range(rows):
-        window = pl.ds(lax.rem(first + offset * r, cols) + r % 2 * room, NEAR)
-        sum_ref[window] = sum_ref[window] + tiles_ref[r * NEAR : (r + 1) * NEAR]
+    for i, r in enumerate(row_order(rows)):
+        window = pl.ds(lax.rem(first + offset * r, cols) + i % 2 * room, NEAR)
+        sum_ref[window] = sum_ref[window] + tiles_ref[i * NEAR : (i + 1) * NEAR]
     line_ref[...] = sum_ref[:cols] + sum_ref[room : room + cols]
     line_ref[: room - cols] = line_ref[: room - cols] + (sum_ref[cols:room] + sum_ref[room + cols :])
 
@@ -74,8 +81,8 @@
     first = first_of()
     twice_ref[:cols] = line_ref[...]
     twice_ref[cols:] = line_ref[:NEAR]
-    for r in range(rows):
-        tiles_ref[r * NEAR : (r + 1) * NEAR] = twice_ref[pl.ds(lax.rem(first + offset * r, cols), NEAR)]
+    for i, r in enumerate(row_order(rows)):
+        tiles_ref[i * NEAR : (i + 1) * NEAR] = twice_ref[pl.ds(lax.rem(first + offset * r, cols), NEAR)]
 
 
 def middle(parts_ref, shear_ref, measured_ref, copies_ref, residual_ref, *, factor):
@@ -116,8 +123,8 @@
     residual_copy.wait()
 
 
-def exchange(values, axes):
-    return lax.all_to_all(values, axes, 0, 0, tiled=True)
+def exchange(values, axes, groups=None):
+    return lax.all_to_all(values, axes, 0, 0, tiled=True, axis_index_groups=groups)
 
 
 def near(values):
@@ -131,6 +138,7 @@
     angles = ray_weights.shape[0]
     factor = 1.0 / math.sqrt(slab_rows * rows)
     f32 = jnp.float32
+    peers = [[r * NEAR + k for r in row_order(rows) for k in range(NEAR)]]
     tiles_of = lambda count: pltpu.VMEM((count, slices, lanes), f32)
     row_of = lambda: lax.axis_index("row")
     angle_of = lambda: lax.axis_index("row") * NEAR + lax.axis_index("near")
@@ -149,6 +157,7 @@
         scratch_shapes=[
             pltpu.VMEM(volume.shape, f32),
             pltpu.VMEM(ray_weights.shape, f32),
+            pltpu.VMEM(ray_weights.shape, f32),
             pltpu.SMEM(shear_offsets.shape, shear_offsets.dtype),
             pltpu.SemaphoreType.DMA((2,)),
             pltpu.SemaphoreType.DMA,
@@ -157,7 +166,7 @@
         ],
         name="sums",
     )(volume, ray_weights, shear_weights, shear_offsets)
-    received = exchange(tilesum.reshape(angles, slices, lanes), ("row", "near"))
+    received = exchange(tilesum.reshape(angles, slices, lanes), ("row", "near"), peers)
     line = pl.pallas_call(
         lambda *refs: push(*refs, first_of=first_of),
         out_shape=tiles_of(cols),
@@ -183,7 +192,7 @@
         scratch_shapes=[tiles_of(cols + NEAR)],
         name="pull",
     )(near(offset), near(returned))
-    arrived = exchange(tiles, ("row", "near")).reshape(angles * slices, lanes)
+    arrived = exchange(tiles, ("row", "near"), peers).reshape(angles * slices, lanes)
     gradient, residual = pl.pallas_call(
         spread_back,
         out_shape=(jax.ShapeDtypeStruct(volume.shape, f32), jax.ShapeDtypeStruct(residual.shape, f32)),

time: 88.6 us -> 84.6 us (0.955)
  blocking collectives: 84.3 us -> 80.3 us
    all_to_all x4, blocking collectives: 84.3 us -> 80.3 us  [exchange(): lax.all_to_all(values, axes, 0, 0, tiled=True, axis_index_groups=groups)]
where the time goes in v6:
time: 84.6 us; the launch traced here: 84.4 us
  blocking collectives  80.3 us (95%)
  Pallas kernels  3.37 us (4%)
    all_to_all x4, blocking collectives, exchange(): lax.all_to_all(values, axes, 0, 0, tiled=True, axis_index_groups=groups)  80.3 us

profile of v6, /device:TPU:1, one launch (start us, length us, event | category | flops | bytes accessed | tf_op | source)
XLA Modules:
  0.0 84.4 jit_solution(9866034159851838198)
XLA Ops:
  0.6 0.0 copy-start
  0.6 1.6 %sums.1 = (f32[512,128]{1,0:T(8,128)S(1)}, bf16[4,128,128]{2,1,0:T(8,128)(2,1)S(1)}, s32[8,128]{1,0:T(8,128)S(1)}, bf16[256,192]{1,0:T(8,128)(2,1)S(1)}) custom-call(f32[8,256,128]{2,1,0:T(8,128)} %refs_0_.1, f32[64,256]{1,0:T(8,128)} %refs_1_.1, bf16[64,128,128]{2,1,0:T(8,128)(2,1)} %refs_2_.2, s32[64]{0:T(128)} %refs_3_.1), custom_call_target="tpu_custom_call" | custom-call | tf_op jit(solution)/shard_map/sums/pallas_call | solution.py:147
  2.3 18.8 %all_to_all.20.refs_1_ = f32[64,8,128]{2,1,0:T(8,128)S(1)} all-to-all(f32[64,8,128]{2,1,0:T(8,128)S(1)} %bitcast.3), channel_id=1, replica_groups={{480,481,482,483,416,417,418,419,352,353,354,355,288,289,290,291,224,22..., dimensions={0} | all-to-all | bytes 524288 | tf_op jit(solution)/shard_map/all_to_all | solution.py:127
  21.1 0.1 push.1
  21.2 27.6 %all_to_all.21.refs_0_ = f32[32,8,128]{2,1,0:T(8,128)S(1)} all-to-all(f32[32,8,128]{2,1,0:T(8,128)S(1)} %push.1), channel_id=1, replica_groups=mesh['row'=16,'far'=8,'near'=4] {'far','near'}, dimensions={0} | all-to-all | bytes 262144 | tf_op jit(solution)/shard_map/all_to_all | solution.py:127
  48.9 0.0 copy-done
  48.9 0.3 middle.1
  49.2 18.1 %all_to_all.22.refs_1_ = f32[32,8,128]{2,1,0:T(8,128)S(1)} all-to-all(f32[32,8,128]{2,1,0:T(8,128)S(1)} %get-tuple-element.13), channel_id=1, replica_groups=mesh['row'=16,'far'=8,'near'=4] {'far','near'}, dimensions={0} | all-to-all | bytes 262144 | tf_op jit(solution)/shard_map/all_to_all | solution.py:127
  67.3 0.1 pull.1
  67.4 15.8 %all_to_all.23 = f32[64,8,128]{2,1,0:T(8,128)S(1)} all-to-all(f32[64,8,128]{2,1,0:T(8,128)S(1)} %pull.1), channel_id=1, replica_groups={{480,481,482,483,416,417,418,419,352,353,354,355,288,289,290,291,224,22..., dimensions={0} | all-to-all | bytes 524288 | tf_op jit(solution)/shard_map/all_to_all | solution.py:127
  83.1 1.2 %spread_back.1 = (f32[8,256,128]{2,1,0:T(8,128)}, f32[4,8,128]{2,1,0:T(8,128)}) custom-call(f32[512,128]{1,0:T(8,128)S(1)} %bitcast.2, bf16[256,192]{1,0:T(8,128)(2,1)S(1)} %get-tuple-element.14.across_ref, f32[4,8,128]{2,1,0:T(8,128)S(1)} %get-tuple-element.15.residual_ref), custom_call_target="tpu_custom_call" | custom-call | tf_op jit(solution)/shard_map/spread_back/pallas_call | solution.py:196
Async XLA Ops:
  0.6 48.3 %copy-start = (f32[4,8,128]{2,1,0:T(8,128)S(1)}, f32[4,8,128]{2,1,0:T(8,128)}, u32[]{:S(2)}) copy-start(f32[4,8,128]{2,1,0:T(8,128)} %refs_2_.3) | copy-start | bytes 49156

commit v7 on v6

--- a/solution.py
+++ b/solution.py
@@ -70,8 +70,11 @@
     for i, r in enumerate(row_order(rows)):
         window = pl.ds(lax.rem(first + offset * r, cols) + i % 2 * room, NEAR)
         sum_ref[window] = sum_ref[window] + tiles_ref[i * NEAR : (i + 1) * NEAR]
-    line_ref[...] = sum_ref[:cols] + sum_ref[room : room + cols]
-    line_ref[: room - cols] = line_ref[: room - cols] + (sum_ref[cols:room] + sum_ref[room + cols :])
+    for c in range(0, cols, NEAR):
+        block = sum_ref[c : c + NEAR] + sum_ref[room + c : room + c + NEAR]
+        if c == 0:
+            block = block + (sum_ref[cols:room] + sum_ref[room + cols :])
+        line_ref[cols - NEAR - c : cols - c] = block
 
 
 def pull(offset_ref, line_ref, tiles_ref, twice_ref, *, first_of):
@@ -79,8 +82,9 @@
     rows = tiles_ref.shape[0] // NEAR
     offset = offset_ref[0, 0]
     first = first_of()
-    twice_ref[:cols] = line_ref[...]
-    twice_ref[cols:] = line_ref[:NEAR]
+    for c in range(0, cols, NEAR):
+        twice_ref[c : c + NEAR] = line_ref[cols - NEAR - c : cols - c]
+    twice_ref[cols:] = line_ref[cols - NEAR :]
     for i, r in enumerate(row_order(rows)):
         tiles_ref[i * NEAR : (i + 1) * NEAR] = twice_ref[pl.ds(lax.rem(first + offset * r, cols), NEAR)]
 
@@ -139,6 +143,7 @@
     factor = 1.0 / math.sqrt(slab_rows * rows)
     f32 = jnp.float32
     peers = [[r * NEAR + k for r in row_order(rows) for k in range(NEAR)]]
+    columns = [[c + k for c in range(cols - NEAR, -1, -NEAR) for k in range(NEAR)]]
     tiles_of = lambda count: pltpu.VMEM((count, slices, lanes), f32)
     row_of = lambda: lax.axis_index("row")
     angle_of = lambda: lax.axis_index("row") * NEAR + lax.axis_index("near")
@@ -175,7 +180,7 @@
         scratch_shapes=[tiles_of(2 * (cols + NEAR))],
         name="push",
     )(near(offset), near(received))
-    parts = exchange(line, ("far", "near"))
+    parts = exchange(line, ("far", "near"), columns)
     answer, residual = pl.pallas_call(
         lambda *refs: middle(*refs, factor=factor),
         out_shape=(tiles_of(cols), tiles_of(NEAR)),
@@ -183,7 +188,7 @@
         out_specs=(VMEM, VMEM),
         name="middle",
     )(near(parts), near(shear), near(measured))
-    returned = exchange(answer, ("far", "near"))
+    returned = exchange(answer, ("far", "near"), columns)
     tiles = pl.pallas_call(
         lambda *refs: pull(*refs, first_of=first_of),
         out_shape=tiles_of(angles),

time: 84.6 us -> 81.7 us (0.966)
  blocking collectives: 80.3 us -> 77.4 us
    all_to_all x4, blocking collectives: 80.3 us -> 77.4 us  [exchange(): lax.all_to_all(values, axes, 0, 0, tiled=True, axis_index_groups=groups)]
where the time goes in v7:
time: 81.7 us; the launch traced here: 81.5 us
  blocking collectives  77.4 us (95%)
  Pallas kernels  3.37 us (4%)
    all_to_all x4, blocking collectives, exchange(): lax.all_to_all(values, axes, 0, 0, tiled=True, axis_index_groups=groups)  77.4 us
    pallas_call x1, Pallas kernels, on_device(): pl.pallas_call(lambda *refs: sums(*refs, row_of=row_of, angle_of=angle_of...  1.63 us

profile of v7, /device:TPU:1, one launch (start us, length us, event | category | flops | bytes accessed | tf_op | source)
XLA Modules:
  0.0 81.5 jit_solution(13442088160689437027)
XLA Ops:
  0.6 0.0 copy-start
  0.6 1.6 %sums.1 = (f32[512,128]{1,0:T(8,128)S(1)}, bf16[4,128,128]{2,1,0:T(8,128)(2,1)S(1)}, s32[8,128]{1,0:T(8,128)S(1)}, bf16[256,192]{1,0:T(8,128)(2,1)S(1)}) custom-call(f32[8,256,128]{2,1,0:T(8,128)} %refs_0_.1, f32[64,256]{1,0:T(8,128)} %refs_1_.1, bf16[64,128,128]{2,1,0:T(8,128)(2,1)} %refs_2_.2, s32[64]{0:T(128)} %refs_3_.1), custom_call_target="tpu_custom_call" | custom-call | tf_op jit(solution)/shard_map/sums/pallas_call | solution.py:152
  2.3 18.8 %all_to_all.20.refs_1_ = f32[64,8,128]{2,1,0:T(8,128)S(1)} all-to-all(f32[64,8,128]{2,1,0:T(8,128)S(1)} %bitcast.3), channel_id=1, replica_groups={{480,481,482,483,416,417,418,419,352,353,354,355,288,289,290,291,224,22..., dimensions={0} | all-to-all | bytes 524288 | tf_op jit(solution)/shard_map/all_to_all | solution.py:131
  21.1 0.1 push.1
  21.2 23.0 %all_to_all.21.refs_0_ = f32[32,8,128]{2,1,0:T(8,128)S(1)} all-to-all(f32[32,8,128]{2,1,0:T(8,128)S(1)} %push.1), channel_id=1, replica_groups={{28,29,30,31,24,25,26,27,20,21,22,23,16,17,18,19,12,13,14,15,8,9,10,11,..., dimensions={0} | all-to-all | bytes 262144 | tf_op jit(solution)/shard_map/all_to_all | solution.py:131
  44.2 0.0 copy-done
  44.2 0.3 middle.1
  44.5 18.6 %all_to_all.22.refs_1_ = f32[32,8,128]{2,1,0:T(8,128)S(1)} all-to-all(f32[32,8,128]{2,1,0:T(8,128)S(1)} %get-tuple-element.13), channel_id=1, replica_groups={{28,29,30,31,24,25,26,27,20,21,22,23,16,17,18,19,12,13,14,15,8,9,10,11,..., dimensions={0} | all-to-all | bytes 262144 | tf_op jit(solution)/shard_map/all_to_all | solution.py:131
  63.1 0.1 pull.1
  63.2 17.1 %all_to_all.23 = f32[64,8,128]{2,1,0:T(8,128)S(1)} all-to-all(f32[64,8,128]{2,1,0:T(8,128)S(1)} %pull.1), channel_id=1, replica_groups={{480,481,482,483,416,417,418,419,352,353,354,355,288,289,290,291,224,22..., dimensions={0} | all-to-all | bytes 524288 | tf_op jit(solution)/shard_map/all_to_all | solution.py:131
  80.2 1.2 %spread_back.1 = (f32[8,256,128]{2,1,0:T(8,128)}, f32[4,8,128]{2,1,0:T(8,128)}) custom-call(f32[512,128]{1,0:T(8,128)S(1)} %bitcast.2, bf16[256,192]{1,0:T(8,128)(2,1)S(1)} %get-tuple-element.14.across_ref, f32[4,8,128]{2,1,0:T(8,128)S(1)} %get-tuple-element.15.residual_ref), custom_call_target="tpu_custom_call" | custom-call | tf_op jit(solution)/shard_map/spread_back/pallas_call | solution.py:201
Async XLA Ops:
  0.6 43.6 %copy-start = (f32[4,8,128]{2,1,0:T(8,128)S(1)}, f32[4,8,128]{2,1,0:T(8,128)}, u32[]{:S(2)}) copy-start(f32[4,8,128]{2,1,0:T(8,128)} %refs_2_.3) | copy-start | bytes 49156

commit v8 on v7

--- a/solution.py
+++ b/solution.py
@@ -14,6 +14,10 @@
 
 def row_order(rows):
     return sorted(range(rows), key=lambda r: (r % 2 == 0, -r))
+
+
+def block_order(blocks):
+    return sorted(range(blocks), key=lambda f: (-min(f, blocks - f), -f if f * 2 == blocks else f))
 
 
 def split(values):
@@ -70,11 +74,12 @@
     for i, r in enumerate(row_order(rows)):
         window = pl.ds(lax.rem(first + offset * r, cols) + i % 2 * room, NEAR)
         sum_ref[window] = sum_ref[window] + tiles_ref[i * NEAR : (i + 1) * NEAR]
-    for c in range(0, cols, NEAR):
+    for i, f in enumerate(block_order(cols // NEAR)):
+        c = f * NEAR
         block = sum_ref[c : c + NEAR] + sum_ref[room + c : room + c + NEAR]
         if c == 0:
             block = block + (sum_ref[cols:room] + sum_ref[room + cols :])
-        line_ref[cols - NEAR - c : cols - c] = block
+        line_ref[i * NEAR : (i + 1) * NEAR] = block
 
 
 def pull(offset_ref, line_ref, tiles_ref, twice_ref, *, first_of):
@@ -82,9 +87,9 @@
     rows = tiles_ref.shape[0] // NEAR
     offset = offset_ref[0, 0]
     first = first_of()
-    for c in range(0, cols, NEAR):
-        twice_ref[c : c + NEAR] = line_ref[cols - NEAR - c : cols - c]
-    twice_ref[cols:] = line_ref[cols - NEAR :]
+    for i, f in enumerate(block_order(cols // NEAR)):
+        twice_ref[f * NEAR : (f + 1) * NEAR] = line_ref[i * NEAR : (i + 1) * NEAR]
+    twice_ref[cols:] = twice_ref[:NEAR]
     for i, r in enumerate(row_order(rows)):
         tiles_ref[i * NEAR : (i + 1) * NEAR] = twice_ref[pl.ds(lax.rem(first + offset * r, cols), NEAR)]
 
@@ -143,7 +148,7 @@
     factor = 1.0 / math.sqrt(slab_rows * rows)
     f32 = jnp.float32
     peers = [[r * NEAR + k for r in row_order(rows) for k in range(NEAR)]]
-    columns = [[c + k for c in range(cols - NEAR, -1, -NEAR) for k in range(NEAR)]]
+    columns = [[f * NEAR + k for f in block_order(cols // NEAR) for k in range(NEAR)]]
     tiles_of = lambda count: pltpu.VMEM((count, slices, lanes), f32)
     row_of = lambda: lax.axis_index("row")
     angle_of = lambda: lax.axis_index("row") * NEAR + lax.axis_index("near")

time: 81.7 us -> 79.5 us (0.973)
  blocking collectives: 77.4 us -> 75.2 us
    all_to_all x4, blocking collectives: 77.4 us -> 75.2 us  [exchange(): lax.all_to_all(values, axes, 0, 0, tiled=True, axis_index_groups=groups)]
where the time goes in v8:
time: 79.5 us; the launch traced here: 79.2 us
  blocking collectives  75.2 us (95%)
  Pallas kernels  3.37 us (4%)
    all_to_all x4, blocking collectives, exchange(): lax.all_to_all(values, axes, 0, 0, tiled=True, axis_index_groups=groups)  75.2 us
    pallas_call x1, Pallas kernels, on_device(): pl.pallas_call(lambda *refs: sums(*refs, row_of=row_of, angle_of=angle_of...  1.63 us

profile of v8, /device:TPU:1, one launch (start us, length us, event | category | flops | bytes accessed | tf_op | source)
XLA Modules:
  0.0 79.2 jit_solution(16591322448979436529)
XLA Ops:
  0.6 0.0 copy-start
  0.6 1.6 %sums.1 = (f32[512,128]{1,0:T(8,128)S(1)}, bf16[4,128,128]{2,1,0:T(8,128)(2,1)S(1)}, s32[8,128]{1,0:T(8,128)S(1)}, bf16[256,192]{1,0:T(8,128)(2,1)S(1)}) custom-call(f32[8,256,128]{2,1,0:T(8,128)} %refs_0_.1, f32[64,256]{1,0:T(8,128)} %refs_1_.1, bf16[64,128,128]{2,1,0:T(8,128)(2,1)} %refs_2_.2, s32[64]{0:T(128)} %refs_3_.1), custom_call_target="tpu_custom_call" | custom-call | tf_op jit(solution)/shard_map/sums/pallas_call | solution.py:157
  2.3 18.8 %all_to_all.20.refs_1_ = f32[64,8,128]{2,1,0:T(8,128)S(1)} all-to-all(f32[64,8,128]{2,1,0:T(8,128)S(1)} %bitcast.3), channel_id=1, replica_groups={{480,481,482,483,416,417,418,419,352,353,354,355,288,289,290,291,224,22..., dimensions={0} | all-to-all | bytes 524288 | tf_op jit(solution)/shard_map/all_to_all | solution.py:136
  21.1 0.1 push.1
  21.2 23.2 %all_to_all.21.refs_0_ = f32[32,8,128]{2,1,0:T(8,128)S(1)} all-to-all(f32[32,8,128]{2,1,0:T(8,128)S(1)} %push.1), channel_id=1, replica_groups={{16,17,18,19,12,13,14,15,20,21,22,23,8,9,10,11,24,25,26,27,4,5,6,7,28,2..., dimensions={0} | all-to-all | bytes 262144 | tf_op jit(solution)/shard_map/all_to_all | solution.py:136
  44.4 0.0 copy-done
  44.4 0.3 middle.1
  44.7 17.6 %all_to_all.22.refs_1_ = f32[32,8,128]{2,1,0:T(8,128)S(1)} all-to-all(f32[32,8,128]{2,1,0:T(8,128)S(1)} %get-tuple-element.13), channel_id=1, replica_groups={{16,17,18,19,12,13,14,15,20,21,22,23,8,9,10,11,24,25,26,27,4,5,6,7,28,2..., dimensions={0} | all-to-all | bytes 262144 | tf_op jit(solution)/shard_map/all_to_all | solution.py:136
  62.4 0.1 pull.1
  62.4 15.5 %all_to_all.23 = f32[64,8,128]{2,1,0:T(8,128)S(1)} all-to-all(f32[64,8,128]{2,1,0:T(8,128)S(1)} %pull.1), channel_id=1, replica_groups={{480,481,482,483,416,417,418,419,352,353,354,355,288,289,290,291,224,22..., dimensions={0} | all-to-all | bytes 524288 | tf_op jit(solution)/shard_map/all_to_all | solution.py:136
  78.0 1.2 %spread_back.1 = (f32[8,256,128]{2,1,0:T(8,128)}, f32[4,8,128]{2,1,0:T(8,128)}) custom-call(f32[512,128]{1,0:T(8,128)S(1)} %bitcast.2, bf16[256,192]{1,0:T(8,128)(2,1)S(1)} %get-tuple-element.14.across_ref, f32[4,8,128]{2,1,0:T(8,128)S(1)} %get-tuple-element.15.residual_ref), custom_call_target="tpu_custom_call" | custom-call | tf_op jit(solution)/shard_map/spread_back/pallas_call | solution.py:206
Async XLA Ops:
  0.6 43.8 %copy-start = (f32[4,8,128]{2,1,0:T(8,128)S(1)}, f32[4,8,128]{2,1,0:T(8,128)}, u32[]{:S(2)}) copy-start(f32[4,8,128]{2,1,0:T(8,128)} %refs_2_.3) | copy-start | bytes 49156
